TPU v7x, 512 devices: a whole 4x8x8 slice. The times are simulated.
512 devices in a mesh: row: 32 (over x, y), col: 16 (over z, core).
Axes of the slice: x: 4, y: 8, z: 8, core: 2. Of those that a mesh axis runs over, the one named last changes fastest.
Arguments:
- fine_blocks: bfloat16 [32, 16, 64, 128, 128], P('row', 'col'), may hold values from -0.5 to 0.5
- fine_rows: int32 [32, 16, 64], P('row', 'col'), may hold values from 0 to 7
- fine_cols: int32 [32, 16, 64], P('row', 'col'), may hold values from 0 to 39
- fine_counts: int32 [32, 16], P('row', 'col'), may hold values from 8 to 64, as said below
- prolong_blocks: bfloat16 [32, 16, 12, 128, 128], P('row', 'col'), may hold values from -1.5 to 1.5
- prolong_codes: int32 [32, 16, 12], P('row', 'col'), may hold values from 0 to 15, as said below
- prolong_counts: int32 [32, 16], P('row', 'col'), may hold values from 6 to 12, as said below
- second_blocks: bfloat16 [32, 16, 2, 128, 128], P('row', 'col'), may hold values from -0.25 to 0.25
- second_aggs: int32 [32, 16, 2], P('row', 'col'), may hold values from 0 to 1
Outputs:
- coarse_one: bfloat16 [32, 16, 2, 5, 2, 128, 128], P('row', 'col')
- coarse_two: float32 [32, 2, 3, 2, 128, 128], P('row')
Inputs may be any that keep to these rules, and one draw needn't show every extreme that they name: Slots from fine_counts[r, c] to 63 are padding and are ignored; in every draw some device has all 64 slots live. `fine_cols`: a source outside the grid of devices contributes nothing. `prolong_codes`: the live slots of one device name distinct blocks. Slots from prolong_counts[r, c] to 11 are padding and are ignored; in every draw some device has all 12 slots live.
All inputs are finite; a program needn't handle non-finite values.
Results may differ from a plain program's by a relative error of at most 0.0057.
Values may be sent and summed in bfloat16 or wider, within the bound.
A program may use at most 64 MiB of HBM per device.

v0:
```python
import jax
import jax.numpy as jnp
from jax import lax
from jax.sharding import PartitionSpec as P

BS = 128
FB = 8
CB = 2
NA = 64
NP = 12
G2 = 2


def padded_2(cells, sides, width):
    for axis, dim in sides:
        count = lax.axis_size(axis)
        ends = count - 1
        head = lax.slice_in_dim(cells, 0, width, axis=dim)
        tail = lax.slice_in_dim(cells, cells.shape[dim] - width, cells.shape[dim], axis=dim)
        cells = jnp.concatenate(
            [
                lax.ppermute(tail, axis, [(i, (i + 1) % count) for i in range(ends)]),
                cells,
                lax.ppermute(head, axis, [((i + 1) % count, i) for i in range(ends)]),
            ],
            axis=dim,
        )
    return cells


def source_stack(padded):
    return jnp.stack([padded[1, 1], padded[1, 0], padded[1, 2], padded[0, 1], padded[2, 1]], axis=0)


def half_product(coarse, sources):
    inside = jnp.einsum(
        "Jsjxy,sjayz->Jaxz", coarse[:, 0:3], sources[0:3], preferred_element_type=jnp.float32
    )
    before = jnp.einsum(
        "Jjxy,jayz->Jaxz", coarse[:, 3], sources[3], preferred_element_type=jnp.float32
    )
    beyond = jnp.einsum(
        "Jjxy,jayz->Jaxz", coarse[:, 4], sources[4], preferred_element_type=jnp.float32
    )
    return jnp.stack([inside, before, beyond], axis=1).astype(jnp.bfloat16)


def per_device(
    fine_blocks,
    fine_rows,
    fine_cols,
    fine_counts,
    prolong_blocks,
    prolong_codes,
    prolong_counts,
    second_blocks,
    second_aggs,
):
    blocks = fine_blocks[0, 0]
    columns = fine_cols[0, 0]
    live_prolong = jnp.arange(NP) < prolong_counts[0, 0]
    placing = (
        (prolong_codes[0, 0][:, None] == jnp.arange(FB * CB)[None, :]) & live_prolong[:, None]
    ).astype(jnp.bfloat16)
    dense_p = jnp.einsum(
        "kq,kxy->qxy", placing, prolong_blocks[0, 0], preferred_element_type=jnp.float32
    ).astype(jnp.bfloat16)
    member = (second_aggs[0, 0][:, None] == jnp.arange(G2)[None, :]).astype(jnp.bfloat16)
    lifted = second_blocks[0, 0][:, None] * member[:, :, None, None]
    padded = padded_2(dense_p.reshape(1, 1, FB * CB, BS, BS), (("row", 0), ("col", 1)), 1)
    rim_lifted = padded_2(lifted.reshape(1, 1, CB, G2, BS, BS), (("row", 0), ("col", 1)), 1)
    near_p = source_stack(padded).reshape(5 * FB, CB, BS, BS)
    fetched = near_p[columns]
    products = jnp.einsum("kxy,kjyz->kjxz", blocks, fetched, preferred_element_type=jnp.float32)
    live_fine = jnp.arange(NA) < fine_counts[0, 0]
    target = fine_rows[0, 0] * 5 + columns // FB
    placing_rows = ((target[:, None] == jnp.arange(5 * FB)[None, :]) & live_fine[:, None]).astype(
        jnp.float32
    )
    summed = jnp.einsum("kt,kjxz->tjxz", placing_rows, products, precision=lax.Precision.HIGHEST)
    fine_product = summed.astype(jnp.bfloat16).reshape(FB, 5, CB, BS, BS)
    own_p = dense_p.reshape(FB, CB, BS, BS)
    coarse_one = jnp.einsum(
        "iJxy,isjxz->Jsjyz", own_p, fine_product, preferred_element_type=jnp.float32
    ).astype(jnp.bfloat16)
    half_prod = half_product(coarse_one, source_stack(rim_lifted))
    own_term = jnp.einsum(
        "Jaxy,Jgbxz->agbyz", lifted, half_prod, preferred_element_type=jnp.float32
    )
    coarse_two = lax.psum(own_term, "col")
    return (coarse_one[None, None], coarse_two[None])


def solution(mesh):
    in_specs = (
        P("row", "col", None, None, None),
        P("row", "col", None),
        P("row", "col", None),
        P("row", "col"),
        P("row", "col", None, None, None),
        P("row", "col", None),
        P("row", "col"),
        P("row", "col", None, None, None),
        P("row", "col", None),
    )
    out_specs = (
        P("row", "col", None, None, None, None, None),
        P("row", None, None, None, None, None),
    )
    return jax.shard_map(
        per_device, mesh=mesh, in_specs=in_specs, out_specs=out_specs, check_vma=False
    )
```

profile of v0, /device:TPU:7, one launch (start us, length us, event | category | flops | bytes accessed | tf_op | source)
XLA Modules:
  0.0 234.4 jit_solution(10222994112995597870)
XLA Ops:
  8.0 2.3 bitcast_dynamic-update-slice_fusion.2
  10.4 3.2 %collective-permute-start = (bf16[1,1,16,128,128]{4,2,3,1,0:T(8,128)(2,1)}, bf16[1,1,16,128,128]{4,2,3,1,0:T(8,128)(2,1)S(1)}, u32[]{:S(2)}, u32[]{:S(2)}) collective-permute-start(bf16[1,1,16,128,128]{4,2,3,1,0:T(8,128)(2,1)} %bitcast.10), channel_id=1, source_target_pairs={{0,16},{16,32},{32,48},{48,64},{64,80},{80,96},{96,112},{112,128},... | collective-permute-start | bytes 1572872 | tf_op jit(solution)/shard_map/ppermute | solution.py:22
  13.6 4.2 %collective-permute-start.1 = (bf16[1,1,16,128,128]{4,2,3,1,0:T(8,128)(2,1)}, bf16[1,1,16,128,128]{4,2,3,1,0:T(8,128)(2,1)S(1)}, u32[]{:S(2)}, u32[]{:S(2)}) collective-permute-start(bf16[1,1,16,128,128]{4,2,3,1,0:T(8,128)(2,1)} %bitcast.10), channel_id=1, source_target_pairs={{16,0},{32,16},{48,32},{64,48},{80,64},{96,80},{112,96},{128,112},... | collective-permute-start | bytes 1572872 | tf_op jit(solution)/shard_map/ppermute | solution.py:24
  17.8 1.0 copy.27
  19.6 7.8 %collective-permute-done = bf16[1,1,16,128,128]{4,2,3,1,0:T(8,128)(2,1)S(1)} collective-permute-done((bf16[1,1,16,128,128]{4,2,3,1,0:T(8,128)(2,1)}, bf16[1,1,16,128,128]{4,2,3,1,0:T(8,128)(2,1)S(1)}, u32[]{:S(2)}, u32[]{:S(2)}) %collective-permute-start) | collective-permute-done | bytes 524320 | tf_op jit(solution)/shard_map/ppermute | solution.py:22
  27.4 1.0 collective-permute-done.1
  28.4 1.2 pad_maximum_fusion
  29.6 5.7 %collective-permute-start.2 = (bf16[3,1,16,128,128]{4,2,3,1,0:T(8,128)(2,1)S(1)}, bf16[3,1,16,128,128]{4,2,3,1,0:T(8,128)(2,1)S(1)}, u32[]{:S(2)}, u32[]{:S(2)}) collective-permute-start(bf16[3,1,16,128,128]{4,2,3,1,0:T(8,128)(2,1)S(1)} %pad_maximum_fusion), channel_id=1, source_target_pairs={{0,1},{1,2},{2,3},{3,4},{4,5},{5,6},{6,7},{7,8},{8,9},{9,10},{10,1... | collective-permute-start | bytes 4718600 | tf_op jit(solution)/shard_map/ppermute | solution.py:22
  35.4 3.0 %collective-permute-start.4 = (bf16[1,1,2,2,128,128]{4,5,2,3,1,0:T(8,128)(2,1)S(1)}, bf16[1,1,2,2,128,128]{4,5,2,3,1,0:T(8,128)(2,1)S(1)}, u32[]{:S(2)}, u32[]{:S(2)}) collective-permute-start(bf16[1,1,2,2,128,128]{4,5,2,3,1,0:T(8,128)(2,1)S(1)} %broadcast_multiply_fusion), channel_id=1, source_target_pairs={{0,16},{16,32},{32,48},{48,64},{64,80},{80,96},{96,112},{112,128},... | collective-permute-start | bytes 393224 | tf_op jit(solution)/shard_map/ppermute | solution.py:22
  38.4 5.0 %collective-permute-start.5 = (bf16[1,1,2,2,128,128]{4,5,2,3,1,0:T(8,128)(2,1)S(1)}, bf16[1,1,2,2,128,128]{4,5,2,3,1,0:T(8,128)(2,1)S(1)}, u32[]{:S(2)}, u32[]{:S(2)}) collective-permute-start(bf16[1,1,2,2,128,128]{4,5,2,3,1,0:T(8,128)(2,1)S(1)} %broadcast_multiply_fusion), channel_id=1, source_target_pairs={{16,0},{32,16},{48,32},{64,48},{80,64},{96,80},{112,96},{128,112},... | collective-permute-start | bytes 393224 | tf_op jit(solution)/shard_map/ppermute | solution.py:24
  43.5 1.9 collective-permute-start.3
  46.9 1.9 collective-permute-start.7
  48.8 3.6 %collective-permute-start.6 = (bf16[3,1,2,2,128,128]{4,5,2,3,1,0:T(8,128)(2,1)S(1)}, bf16[3,1,2,2,128,128]{4,5,2,3,1,0:T(8,128)(2,1)S(1)}, u32[]{:S(2)}, u32[]{:S(2)}) collective-permute-start(bf16[3,1,2,2,128,128]{4,5,2,3,1,0:T(8,128)(2,1)S(1)} %pad_maximum_fusion.1), channel_id=1, source_target_pairs={{0,1},{1,2},{2,3},{3,4},{4,5},{5,6},{6,7},{7,8},{8,9},{9,10},{10,1... | collective-permute-start | bytes 1179656 | tf_op jit(solution)/shard_map/ppermute | solution.py:22
  52.5 16.9 %collective-permute-done.7 = bf16[3,1,2,2,128,128]{4,5,2,3,1,0:T(8,128)(2,1)S(1)} collective-permute-done((bf16[3,1,2,2,128,128]{4,5,2,3,1,0:T(8,128)(2,1)S(1)}, bf16[3,1,2,2,128,128]{4,5,2,3,1,0:T(8,128)(2,1)S(1)}, u32[]{:S(2)}, u32[]{:S(2)}) %collective-permute-start.7) | collective-permute-done | bytes 393248 | tf_op jit(solution)/shard_map/ppermute | solution.py:24
  71.1 2.2 copy.23
  73.2 4.8 %gather_fusion = bf16[64,2,128,128]{3,2,1,0:T(8,128)(2,1)} fusion(bf16[40,2,128,128]{3,2,1,0:T(8,128)(2,1)} %bitcast.175, s32[1024]{0:T(1024)S(1)} %pad_clamp_fusion), kind=kCustom, calls=%fused_computation | custom fusion | bytes 8388864 | tf_op jit(solution)/shard_map/gather | solution.py:73
  78.0 6.7 %fusion.4 = f32[64,2,128,128]{3,2,1,0:T(8,128)} fusion(bf16[64,2,128,128]{3,2,1,0:T(8,128)(2,1)} %gather_fusion, bf16[1,1,64,128,128]{4,3,2,1,0:T(8,128)(2,1)S(1)} %copy-done), kind=kOutput, calls=%fused_computation.5 | convolution fusion | flops 536870912 | bytes 14680064 | tf_op jit(solution)/shard_map/kxy,kjyz->kjxz/dot_general | solution.py:74
  84.8 8.7 %copy.36 = f32[64,2,128,128]{2,0,3,1:T(8,128)} copy(f32[64,2,128,128]{3,2,1,0:T(8,128)} %fusion.4) | data formatting | bytes 16777216 | tf_op jit(solution)/shard_map/kxy,kjyz->kjxz/dot_general | solution.py:74
  93.5 7.4 %fusion.6 = bf16[40,2,128,128]{3,0,2,1:T(8,128)(2,1)S(1)} fusion(f32[64,2,128,128]{2,0,3,1:T(8,128)} %copy.36, s32[64]{0:T(128)S(1)} %bitcast_add_fusion, pred[64]{0:T(512)(128)(4,1)S(1)} %iota_compare_fusion.3), kind=kOutput, calls=%fused_computation.7 | convolution fusion | flops 1007948800 | bytes 11010368 | tf_op jit(solution)/shard_map/kt,kjxz->tjxz/dot_general | solution.py:80
  101.5 2.0 fusion.12
  104.4 1.2 convolution_bitcast_fusion
  105.6 1.1 copy.33
  106.7 118.6 %all-reduce.2.cloned.1.call-done = f32[1,2,3,2,128,128]{4,5,1,3,2,0:T(8,128)} async-done(((f32[1,2,3,2,128,128]{4,5,1,3,2,0:T(8,128)}), f32[1,2,3,2,128,128]{4,5,1,3,2,0:T(8,128)}) %all-reduce.2.cloned.1.call-update) | async-done | bytes 786448 | tf_op jit(solution)/shard_map/psum | solution.py:90
  225.3 2.3 copy.34
  (42 shorter events, 4.8 us)
Async XLA Ops:
  7.2 70.9 %copy-start = (bf16[1,1,64,128,128]{4,3,2,1,0:T(8,128)(2,1)S(1)}, bf16[1,1,64,128,128]{4,3,2,1,0:T(8,128)(2,1)}, u32[]{:S(2)}) copy-start(bf16[1,1,64,128,128]{4,3,2,1,0:T(8,128)(2,1)} %param.9) | copy-start | bytes 6291460
  7.2 218.1 %all-reduce.2.cloned.1.call-start = ((), (), s32[]{:S(2)}) async-start(), calls=%async_computation | async-start | bytes 1572864 | tf_op jit(solution)/shard_map/psum | solution.py:90
  8.0 38.7 %copy-start.6 = (s32[1,1,64]{2,1,0:T(1,128)S(1)}, s32[1,1,64]{2,1,0:T(1,128)}, u32[]{:S(2)}) copy-start(s32[1,1,64]{2,1,0:T(1,128)} %param.10) | copy-start | bytes 772
  8.0 38.7 %copy-start.7 = (s32[1,1,64]{2,1,0:T(1,128)S(1)}, s32[1,1,64]{2,1,0:T(1,128)}, u32[]{:S(2)}) copy-start(s32[1,1,64]{2,1,0:T(1,128)} %param.11) | copy-start | bytes 772
  10.4 17.0 %collective-permute-start = (bf16[1,1,16,128,128]{4,2,3,1,0:T(8,128)(2,1)}, bf16[1,1,16,128,128]{4,2,3,1,0:T(8,128)(2,1)S(1)}, u32[]{:S(2)}, u32[]{:S(2)}) collective-permute-start(bf16[1,1,16,128,128]{4,2,3,1,0:T(8,128)(2,1)} %bitcast.10), channel_id=1, source_target_pairs={{0,16},{16,32},{32,48},{48,64},{64,80},{80,96},{96,112},{112,128},... | collective-permute-start | bytes 1572872 | tf_op jit(solution)/shard_map/ppermute | solution.py:22
  13.6 14.8 %collective-permute-start.1 = (bf16[1,1,16,128,128]{4,2,3,1,0:T(8,128)(2,1)}, bf16[1,1,16,128,128]{4,2,3,1,0:T(8,128)(2,1)S(1)}, u32[]{:S(2)}, u32[]{:S(2)}) collective-permute-start(bf16[1,1,16,128,128]{4,2,3,1,0:T(8,128)(2,1)} %bitcast.10), channel_id=1, source_target_pairs={{16,0},{32,16},{48,32},{64,48},{80,64},{96,80},{112,96},{128,112},... | collective-permute-start | bytes 1572872 | tf_op jit(solution)/shard_map/ppermute | solution.py:24
  18.7 52.0 %copy-start.1 = (bf16[5,16,128,128]{3,1,2,0:T(8,128)(2,1)S(1)}, bf16[5,16,128,128]{3,1,2,0:T(8,128)(2,1)}, u32[]{:S(2)}) copy-start(bf16[5,16,128,128]{3,1,2,0:T(8,128)(2,1)} %get-tuple-element.6) | copy-start | bytes 7864324
  29.6 41.1 %collective-permute-start.2 = (bf16[3,1,16,128,128]{4,2,3,1,0:T(8,128)(2,1)S(1)}, bf16[3,1,16,128,128]{4,2,3,1,0:T(8,128)(2,1)S(1)}, u32[]{:S(2)}, u32[]{:S(2)}) collective-permute-start(bf16[3,1,16,128,128]{4,2,3,1,0:T(8,128)(2,1)S(1)} %pad_maximum_fusion), channel_id=1, source_target_pairs={{0,1},{1,2},{2,3},{3,4},{4,5},{5,6},{6,7},{7,8},{8,9},{9,10},{10,1... | collective-permute-start | bytes 4718600 | tf_op jit(solution)/shard_map/ppermute | solution.py:22
  35.4 11.4 %collective-permute-start.4 = (bf16[1,1,2,2,128,128]{4,5,2,3,1,0:T(8,128)(2,1)S(1)}, bf16[1,1,2,2,128,128]{4,5,2,3,1,0:T(8,128)(2,1)S(1)}, u32[]{:S(2)}, u32[]{:S(2)}) collective-permute-start(bf16[1,1,2,2,128,128]{4,5,2,3,1,0:T(8,128)(2,1)S(1)} %broadcast_multiply_fusion), channel_id=1, source_target_pairs={{0,16},{16,32},{32,48},{48,64},{64,80},{80,96},{96,112},{112,128},... | collective-permute-start | bytes 393224 | tf_op jit(solution)/shard_map/ppermute | solution.py:22
  38.4 8.4 %collective-permute-start.5 = (bf16[1,1,2,2,128,128]{4,5,2,3,1,0:T(8,128)(2,1)S(1)}, bf16[1,1,2,2,128,128]{4,5,2,3,1,0:T(8,128)(2,1)S(1)}, u32[]{:S(2)}, u32[]{:S(2)}) collective-permute-start(bf16[1,1,2,2,128,128]{4,5,2,3,1,0:T(8,128)(2,1)S(1)} %broadcast_multiply_fusion), channel_id=1, source_target_pairs={{16,0},{32,16},{48,32},{64,48},{80,64},{96,80},{112,96},{128,112},... | collective-permute-start | bytes 393224 | tf_op jit(solution)/shard_map/ppermute | solution.py:24
  43.5 27.4 %collective-permute-start.3 = (bf16[3,1,16,128,128]{4,2,3,1,0:T(8,128)(2,1)S(1)}, bf16[3,1,16,128,128]{4,2,3,1,0:T(8,128)(2,1)S(1)}, u32[]{:S(2)}, u32[]{:S(2)}) collective-permute-start(bf16[3,1,16,128,128]{4,2,3,1,0:T(8,128)(2,1)S(1)} %pad_maximum_fusion), channel_id=1, source_target_pairs={{1,0},{2,1},{3,2},{4,3},{5,4},{6,5},{7,6},{8,7},{9,8},{10,9},{11,1... | collective-permute-start | bytes 4718600 | tf_op jit(solution)/shard_map/ppermute | solution.py:24
  46.9 22.5 %collective-permute-start.7 = (bf16[3,1,2,2,128,128]{4,5,2,3,1,0:T(8,128)(2,1)S(1)}, bf16[3,1,2,2,128,128]{4,5,2,3,1,0:T(8,128)(2,1)S(1)}, u32[]{:S(2)}, u32[]{:S(2)}) collective-permute-start(bf16[3,1,2,2,128,128]{4,5,2,3,1,0:T(8,128)(2,1)S(1)} %pad_maximum_fusion.1), channel_id=1, source_target_pairs={{1,0},{2,1},{3,2},{4,3},{5,4},{6,5},{7,6},{8,7},{9,8},{10,9},{11,1... | collective-permute-start | bytes 1179656 | tf_op jit(solution)/shard_map/ppermute | solution.py:24
  48.8 21.3 %collective-permute-start.6 = (bf16[3,1,2,2,128,128]{4,5,2,3,1,0:T(8,128)(2,1)S(1)}, bf16[3,1,2,2,128,128]{4,5,2,3,1,0:T(8,128)(2,1)S(1)}, u32[]{:S(2)}, u32[]{:S(2)}) collective-permute-start(bf16[3,1,2,2,128,128]{4,5,2,3,1,0:T(8,128)(2,1)S(1)} %pad_maximum_fusion.1), channel_id=1, source_target_pairs={{0,1},{1,2},{2,3},{3,4},{4,5},{5,6},{6,7},{7,8},{8,9},{9,10},{10,1... | collective-permute-start | bytes 1179656 | tf_op jit(solution)/shard_map/ppermute | solution.py:22
  101.5 2.0 copy-start.2
  101.5 2.0 copy-start.3
  101.5 2.0 copy-start.4
  103.5 0.8 copy-start.5
Sparse Core Ops, SparseCore 0:
  105.7 119.4 all-reduce.1
where the time goes:
time: 236 us; the launch traced here: 234 us
  waiting for transfers between devices  144 us (61%)
  starting transfers between devices  28.6 us (12%)
  local copies, waits for them, and re-layouts  22.5 us (10%)
  matrix products  20.3 us (9%)
  between operations  15.8 us (7%)
  other arithmetic  2.91 us (1%)
    psum x1, waiting for transfers between devices, per_device(): coarse_two = lax.psum(own_term, 'col')  119 us
    ppermute x4, waiting for transfers between devices, padded_2(): lax.ppermute(head, axis, [((i + 1) % count, i) for i in range(ends)])  17.9 us
    ppermute x4, starting transfers between devices, padded_2(): lax.ppermute(tail, axis, [(i, (i + 1) % count) for i in range(ends)])  15.6 us
    ppermute x4, starting transfers between devices, padded_2(): lax.ppermute(head, axis, [((i + 1) % count, i) for i in range(ends)])  13 us
    dot_general x1, local copies, waits for them, and re-layouts, per_device(): jnp.einsum('kxy,kjyz->kjxz', blocks, fetched, preferred_element_type=jnp....  8.72 us
    ppermute x4, waiting for transfers between devices, padded_2(): lax.ppermute(tail, axis, [(i, (i + 1) % count) for i in range(ends)])  7.84 us
    dot_general x1, matrix products, per_device(): jnp.einsum('kt,kjxz->tjxz', placing_rows, products, precision=lax.Precisi...  7.36 us
    dot_general x1, matrix products, per_device(): jnp.einsum('kxy,kjyz->kjxz', blocks, fetched, preferred_element_type=jnp....  6.71 us
  transfers between devices with their start and end apart: 9, of which 4 were waited for; matrix products, arithmetic and copies ran while one was open for 2% of the time, Pallas kernels for 0%

commit v1 on v0

v1 whole, which is shorter than its diff:
```python
import jax
import jax.numpy as jnp
from jax import lax
from jax.experimental import pallas as pl
from jax.experimental.pallas import tpu as pltpu
from jax.sharding import PartitionSpec as P

BS = 128
FB = 8
CB = 2
NA = 64
NP = 12
G2 = 2
NR = 32
NC = 16
CHIPS = NC // 2
W2 = CB * BS
BF = jnp.bfloat16
F32 = jnp.float32
MESH = pl.DeviceIdType.MESH
HALF = (BS, 2 * BS)
REACH = (4, 3, 5, 2, 6, 1, 7)


def dot(a, b):
    return jnp.dot(a, b, preferred_element_type=F32)


def kernel(
    a_hbm,
    rows_hbm,
    cols_hbm,
    fcount_hbm,
    p_hbm,
    codes_hbm,
    pcount_hbm,
    l_hbm,
    aggs_hbm,
    one_ref,
    two_ref,
    a_buf,
    p_0,
    p_1,
    p_2,
    p_3,
    p_4,
    l_buf,
    rows_s,
    cols_v,
    fcount_v,
    codes_v,
    pcount_v,
    aggs_s,
    table_v,
    table_s,
    near_v,
    near_s,
    pt,
    run,
    wide,
    lifted,
    lifted_t,
    c1,
    give_e,
    give_l,
    take_e,
    take_l,
    part_e,
    part_l,
    rs_e,
    rs_l,
    all_e,
    all_l,
    load_sem,
    halo_send,
    halo_recv,
    pair_send,
    pair_recv,
    rs_send,
    rs_recv,
    ag_send,
    ag_recv,
    fw_send,
    fw_recv,
    reach_sem,
):
    p_bufs = (p_0, p_1, p_2, p_3, p_4)
    row = lax.axis_index("row")
    col = lax.axis_index("col")
    chip = col // 2
    core = col % 2
    partner = 2 * chip + 1 - core

    def at(dr, dc):
        return {"row": (row + dr + NR) % NR, "col": (col + dc + NC) % NC}

    sources = ((0, -1), (0, 1), (-1, 0), (1, 0))

    barrier = pltpu.get_barrier_semaphore()
    for dr, dc in sources:
        pl.semaphore_signal(barrier, inc=1, device_id=at(dr, dc), device_id_type=MESH)

    loads = [
        pltpu.make_async_copy(cols_hbm, cols_v, load_sem.at[0]),
        pltpu.make_async_copy(fcount_hbm, fcount_v, load_sem.at[1]),
        pltpu.make_async_copy(codes_hbm, codes_v.at[0], load_sem.at[2]),
        pltpu.make_async_copy(pcount_hbm, pcount_v.at[0], load_sem.at[3]),
        pltpu.make_async_copy(aggs_hbm, aggs_s.at[0], load_sem.at[4]),
        pltpu.make_async_copy(rows_hbm, rows_s, load_sem.at[5]),
        pltpu.make_async_copy(p_hbm, p_0.at[pl.ds(0, NP)], load_sem.at[6]),
        pltpu.make_async_copy(l_hbm, l_buf.at[0], load_sem.at[7]),
        pltpu.make_async_copy(a_hbm, a_buf, load_sem.at[8]),
    ]
    for load in loads:
        load.start()
    for s in range(5):
        p_bufs[s][NP] = jnp.zeros((BS, BS), BF)
    run[NA] = jnp.zeros((W2, BS), F32)

    pl.semaphore_wait(barrier, 4)

    def halo(s, item):
        src, dst = (
            (codes_hbm, codes_v.at[s]),
            (pcount_hbm, pcount_v.at[s]),
            (aggs_hbm, aggs_s.at[s]),
            (p_hbm, p_bufs[s].at[pl.ds(0, NP)]),
            (l_hbm, l_buf.at[s]),
        )[item]
        dr, dc = sources[s - 1]
        return pltpu.make_async_remote_copy(
            src_ref=src,
            dst_ref=dst,
            send_sem=halo_send.at[s - 1, item],
            recv_sem=halo_recv.at[s - 1, item],
            device_id=at(-dr, -dc),
            device_id_type=MESH,
        )

    order = (3, 4, 1, 2)
    for items in ((0, 1, 2), (3,), (4,)):
        for item in items:
            for s in order:
                halo(s, item).start()

    def widen(step, slot):
        sem = reach_sem.at[slot]
        for sign in (-1, 1):
            pl.semaphore_signal(sem, inc=1, device_id=at(0, sign * step), device_id_type=MESH)
        pl.semaphore_wait(sem, 2)

    for load in loads[:4]:
        load.wait()
    sub = lax.broadcasted_iota(jnp.int32, (BS, BS), 0)
    lane = lax.broadcasted_iota(jnp.int32, (BS, BS), 1)

    def down(vector, length):
        wide_row = jnp.broadcast_to(vector, (length, length))
        diag = sub[:length, :length] == lane[:length, :length]
        return jnp.max(jnp.where(diag, wide_row, -1), axis=1, keepdims=True)

    def pick(match, length, missing):
        best = jnp.max(jnp.where(match, sub[:length], -1), axis=0, keepdims=True)
        return jnp.where(best < 0, missing, best)

    cols = cols_v[...].reshape(1, NA)
    cols_down = down(cols, NA)
    live = sub[:NA] < fcount_v[...]
    cols_wide = jnp.concatenate([cols, cols], axis=1)
    table_v[0:1] = pick(
        (cols_down == cols_wide) & (sub[:NA] < lane[:NA]) & live, NA, NA
    )
    table_v[1:2] = pick((cols_down == lane[:NA]) & live, NA, NA)

    def place(s):
        codes = codes_v[s].reshape(1, NP)
        diag = sub[:16, :NP] == lane[:16, :NP]
        codes_down = jnp.max(
            jnp.where(diag, jnp.broadcast_to(codes, (16, NP)), -1), axis=1, keepdims=True
        )
        return pick((codes_down == lane[:16]) & (sub[:16] < pcount_v[s]), 16, NP)

    table_v[2:3] = place(0)
    send_table = pltpu.make_async_copy(table_v, table_s, load_sem.at[9])
    send_table.start()
    widen(1, 0)
    send_table.wait()
    loads[5].wait()
    loads[6].wait()

    def turn(i, carry):
        for coarse in range(CB):
            slot = table_s[2, i * CB + coarse]
            pt[i, pl.ds(coarse * BS, BS), :] = p_0[slot].T
        return carry

    lax.fori_loop(0, FB, turn, 0)
    loads[8].wait()

    def slots(step, carry):
        for inner in range(4):
            k = step * 4 + inner
            run[k] = dot(pt[rows_s[0, 0, k]], a_buf[k]) + run[table_s[0, k]]
        return carry

    lax.fori_loop(0, NA // 4, slots, 0)
    widen(2, 1)

    def widen_rows(s, carry):
        for m in range(FB):
            slot = table_s[1, s * FB + m]
            wide[s, m // 2, :, pl.ds((m % 2) * BS, BS)] = run[slot].astype(BF)
        return carry

    lax.fori_loop(0, 5, widen_rows, 0)
    widen(4, 2)

    for s in range(1, 5):
        for item in range(3):
            halo(s, item).wait_recv()
    for s in range(1, 5):
        near_v[s : s + 1] = place(s)
    near_v[0:1] = table_v[2:3]
    send_near = pltpu.make_async_copy(near_v, near_s, load_sem.at[10])
    send_near.start()
    loads[4].wait()
    loads[7].wait()

    def lift(s):
        for j in range(CB):
            block = l_buf[s, j]
            for a in range(G2):
                kept = jnp.where(aggs_s[s, 0, 0, j] == a, block, jnp.zeros_like(block))
                lifted[s, pl.ds(j * BS, BS), pl.ds(a * BS, BS)] = kept

    lift(0)
    lifted_t[...] = lifted[0].T
    send_near.wait()

    inside = (None, col > 0, col < NC - 1, row > 0, row < NR - 1)

    def level_one(s):
        total = jnp.zeros((W2, W2), F32)
        for pair in range(FB // 2):
            right = jnp.concatenate(
                [
                    jnp.concatenate(
                        [p_bufs[s][near_s[s, (2 * pair + low) * CB + j]] for j in range(CB)], axis=1
                    )
                    for low in range(2)
                ],
                axis=0,
            )
            total += dot(wide[s, pair], right)
        if inside[s] is not None:
            total = jnp.where(inside[s], total, jnp.zeros_like(total))
        result = total.astype(BF)
        for coarse in range(CB):
            for j in range(CB):
                one_ref[coarse, s, j] = result[
                    coarse * BS : (coarse + 1) * BS, j * BS : (j + 1) * BS
                ]
        return result

    def half_term(firsts):
        total = jnp.zeros((W2, W2), F32)
        for s, result in firsts:
            total += dot(result, lifted[s])
        return dot(lifted_t[...], total.astype(BF))

    gives, takes, parts = (give_e, give_l), (take_e, take_l), (part_e, part_l)
    shares, whole = (rs_e, rs_l), (all_e, all_l)

    def pair_copy(w):
        return pltpu.make_async_remote_copy(
            src_ref=gives[w].at[1 - core],
            dst_ref=takes[w],
            send_sem=pair_send.at[w],
            recv_sem=pair_recv.at[w],
            device_id={"row": row, "col": partner},
            device_id_type=MESH,
        )

    def peer(dz):
        return {"row": row, "col": 2 * ((chip + dz) % CHIPS) + core}

    def rs_copy(w, dz):
        return pltpu.make_async_remote_copy(
            src_ref=parts[w].at[(chip + dz) % CHIPS],
            dst_ref=shares[w].at[dz],
            send_sem=rs_send.at[w, dz],
            recv_sem=rs_recv.at[w, dz],
            device_id=peer(dz),
            device_id_type=MESH,
        )

    def ag_copy(w, dz):
        return pltpu.make_async_remote_copy(
            src_ref=whole[w].at[core, chip],
            dst_ref=whole[w].at[core, chip],
            send_sem=ag_send.at[w, dz],
            recv_sem=ag_recv.at[w, dz],
            device_id=peer(dz),
            device_id_type=MESH,
        )

    def ag_arrival(w, dz):
        landing = whole[w].at[core, (chip - dz + CHIPS) % CHIPS]
        return pltpu.make_async_remote_copy(
            src_ref=landing,
            dst_ref=landing,
            send_sem=ag_send.at[w, dz],
            recv_sem=ag_recv.at[w, dz],
            device_id=peer(dz),
            device_id_type=MESH,
        )

    def forward(w, dz):
        piece = whole[w].at[core, (chip - dz + CHIPS) % CHIPS]
        return pltpu.make_async_remote_copy(
            src_ref=piece,
            dst_ref=piece,
            send_sem=fw_send.at[w, dz],
            recv_sem=fw_recv.at[w, dz],
            device_id={"row": row, "col": partner},
            device_id_type=MESH,
        )

    def forward_arrival(w, dz):
        piece = whole[w].at[1 - core, (chip - dz + CHIPS) % CHIPS]
        return pltpu.make_async_remote_copy(
            src_ref=piece,
            dst_ref=piece,
            send_sem=fw_send.at[w, dz],
            recv_sem=fw_recv.at[w, dz],
            device_id={"row": row, "col": partner},
            device_id_type=MESH,
        )

    def scatter(w):
        pair_copy(w).wait_recv()
        total = gives[w][core].astype(F32) + takes[w][...].astype(F32)
        parts[w][...] = total.astype(BF).reshape(CHIPS, HALF[w] // CHIPS, W2)
        for dz in REACH:
            rs_copy(w, dz).start()

    def gather(w):
        total = parts[w][chip].astype(F32)
        for dz in REACH[::-1]:
            rs_copy(w, dz).wait_recv()
            total += shares[w][dz].astype(F32)
        whole[w][core, chip] = total.astype(BF)
        for dz in REACH:
            ag_copy(w, dz).start()
        forward(w, 0).start()

    def hand_over(w):
        for dz in REACH[::-1]:
            ag_arrival(w, dz).wait_recv()
            forward(w, dz).start()

    firsts = [(0, level_one(0))]
    for s in (1, 2):
        halo(s, 3).wait_recv()
        firsts.append((s, level_one(s)))
    for s in (1, 2):
        halo(s, 4).wait_recv()
        lift(s)
    early = half_term(firsts).astype(BF)
    for side in range(2):
        give_e[side] = early[side * BS : (side + 1) * BS]
    pair_copy(0).start()
    scatter(0)

    for s in (3, 4):
        halo(s, 3).wait_recv()
        result = level_one(s)
        halo(s, 4).wait_recv()
        lift(s)
        give_l[s - 3] = half_term([(s, result)]).astype(BF)
    pair_copy(1).start()
    gather(0)
    scatter(1)
    hand_over(0)
    gather(1)
    hand_over(1)
    for w in range(2):
        for dz in range(CHIPS):
            forward_arrival(w, dz).wait_recv()
        size = HALF[w] // CHIPS
        for side in range(2):
            for piece in range(CHIPS):
                block = whole[w][side, piece].astype(F32)
                if w == 0:
                    a, g, y = side, 0, piece * size
                else:
                    a, g, y = piece // 4, 1 + side, (piece % 4) * size
                for b in range(G2):
                    two_ref[a, g, b, pl.ds(y, size), :] = block[:, b * BS : (b + 1) * BS]

    for s in range(1, 5):
        for item in range(5):
            halo(s, item).wait_send()
    for w in range(2):
        pair_copy(w).wait_send()
        for dz in REACH:
            rs_copy(w, dz).wait_send()
            ag_copy(w, dz).wait_send()
        for dz in range(CHIPS):
            forward(w, dz).wait_send()


def per_device(
    fine_blocks,
    fine_rows,
    fine_cols,
    fine_counts,
    prolong_blocks,
    prolong_codes,
    prolong_counts,
    second_blocks,
    second_aggs,
):
    any_spec = pl.BlockSpec(memory_space=pl.ANY)
    vmem = pl.BlockSpec(memory_space=pltpu.VMEM)
    dma = pltpu.SemaphoreType.DMA
    one, two = pl.pallas_call(
        kernel,
        name="galerkin",
        out_shape=(
            jax.ShapeDtypeStruct((CB, 5, CB, BS, BS), BF),
            jax.ShapeDtypeStruct((G2, 3, G2, BS, BS), F32),
        ),
        in_specs=[any_spec] * 9,
        out_specs=(vmem, vmem),
        scratch_shapes=[
            pltpu.VMEM((NA, BS, BS), BF),
            *[pltpu.VMEM((NP + 1, BS, BS), BF)] * 5,
            pltpu.VMEM((5, CB, BS, BS), BF),
            pltpu.SMEM((1, 1, NA), jnp.int32),
            pltpu.VMEM((1, 1, NA), jnp.int32),
            pltpu.VMEM((1, 1), jnp.int32),
            pltpu.VMEM((5, 1, 1, NP), jnp.int32),
            pltpu.VMEM((5, 1, 1), jnp.int32),
            pltpu.SMEM((5, 1, 1, CB), jnp.int32),
            pltpu.VMEM((8, BS), jnp.int32),
            pltpu.SMEM((8, BS), jnp.int32),
            pltpu.VMEM((8, BS), jnp.int32),
            pltpu.SMEM((8, BS), jnp.int32),
            pltpu.VMEM((FB, W2, BS), BF),
            pltpu.VMEM((NA + 1, W2, BS), F32),
            pltpu.VMEM((5, FB // 2, W2, W2), BF),
            pltpu.VMEM((5, W2, W2), BF),
            pltpu.VMEM((W2, W2), BF),
            pltpu.VMEM((8, BS), BF),
            pltpu.VMEM((2, HALF[0], W2), BF),
            pltpu.VMEM((2, HALF[1], W2), BF),
            pltpu.VMEM((HALF[0], W2), BF),
            pltpu.VMEM((HALF[1], W2), BF),
            pltpu.VMEM((CHIPS, HALF[0] // CHIPS, W2), BF),
            pltpu.VMEM((CHIPS, HALF[1] // CHIPS, W2), BF),
            pltpu.VMEM((CHIPS, HALF[0] // CHIPS, W2), BF),
            pltpu.VMEM((CHIPS, HALF[1] // CHIPS, W2), BF),
            pltpu.VMEM((2, CHIPS, HALF[0] // CHIPS, W2), BF),
            pltpu.VMEM((2, CHIPS, HALF[1] // CHIPS, W2), BF),
            dma((11,)),
            dma((4, 5)),
            dma((4, 5)),
            dma((2,)),
            dma((2,)),
            dma((2, CHIPS)),
            dma((2, CHIPS)),
            dma((2, CHIPS)),
            dma((2, CHIPS)),
            dma((2, CHIPS)),
            dma((2, CHIPS)),
            pltpu.SemaphoreType.REGULAR((3,)),
        ],
        compiler_params=pltpu.CompilerParams(
            collective_id=0, has_side_effects=True, vmem_limit_bytes=48 << 20
        ),
    )(
        fine_blocks[0, 0],
        fine_rows,
        fine_cols,
        fine_counts,
        prolong_blocks[0, 0],
        prolong_codes,
        prolong_counts,
        second_blocks[0, 0],
        second_aggs,
    )
    return (one[None, None], two[None])


def solution(mesh):
    in_specs = (
        P("row", "col", None, None, None),
        P("row", "col", None),
        P("row", "col", None),
        P("row", "col"),
        P("row", "col", None, None, None),
        P("row", "col", None),
        P("row", "col"),
        P("row", "col", None, None, None),
        P("row", "col", None),
    )
    out_specs = (
        P("row", "col", None, None, None, None, None),
        P("row", None, None, None, None, None),
    )
    return jax.shard_map(
        per_device, mesh=mesh, in_specs=in_specs, out_specs=out_specs, check_vma=False
    )
```

time: 236 us -> 57.2 us (0.24)
  the two profiles are of different devices: /device:TPU:7 before, /device:TPU:1 now
where the time goes in v1:
time: 57.2 us; the launch traced here: 56.9 us
  Pallas kernels  47.2 us (83%)
  local copies, waits for them, and re-layouts  7.76 us (14%)
  between operations  1.95 us (3%)
    pallas_call x1, Pallas kernels, per_device(): pl.pallas_call(kernel, name='galerkin', out_shape=(jax.ShapeDtypeStruct((...  47.2 us
    unnamed x16, local copies, waits for them, and re-layouts  7.76 us

profile of v1, /device:TPU:1, one launch (start us, length us, event | category | flops | bytes accessed | tf_op | source)
XLA Modules:
  0.0 56.9 jit_solution(8312651886328217762)
XLA Ops:
  1.9 0.0 copy-start
  1.9 1.6 %copy-done = bf16[1,1,64,128,128]{4,3,2,1,0:T(8,128)(2,1)S(1)} copy-done((bf16[1,1,64,128,128]{4,3,2,1,0:T(8,128)(2,1)S(1)}, bf16[1,1,64,128,128]{4,3,2,1,0:T(8,128)(2,1)}, u32[]{:S(2)}) %copy-start) | copy-done | bytes 2097176
  3.5 0.0 copy-start.1
  3.5 1.0 %copy-done.1 = bf16[1,1,12,128,128]{4,3,2,1,0:T(8,128)(2,1)S(1)} copy-done((bf16[1,1,12,128,128]{4,3,2,1,0:T(8,128)(2,1)S(1)}, bf16[1,1,12,128,128]{4,3,2,1,0:T(8,128)(2,1)}, u32[]{:S(2)}) %copy-start.1) | copy-done | bytes 393240
  4.5 0.0 copy-start.2
  4.5 0.8 %copy-done.2 = bf16[1,1,2,128,128]{4,3,2,1,0:T(8,128)(2,1)S(1)} copy-done((bf16[1,1,2,128,128]{4,3,2,1,0:T(8,128)(2,1)S(1)}, bf16[1,1,2,128,128]{4,3,2,1,0:T(8,128)(2,1)}, u32[]{:S(2)}) %copy-start.2) | copy-done | bytes 65560
  5.4 0.0 copy-start.3
  5.4 0.7 %copy-done.3 = s32[1,1,64]{2,1,0:T(1,128)S(1)} copy-done((s32[1,1,64]{2,1,0:T(1,128)S(1)}, s32[1,1,64]{2,1,0:T(1,128)}, u32[]{:S(2)}) %copy-start.3) | copy-done | bytes 280
  6.0 0.0 copy-start.4
  6.0 0.7 %copy-done.4 = s32[1,1,64]{2,1,0:T(1,128)S(1)} copy-done((s32[1,1,64]{2,1,0:T(1,128)S(1)}, s32[1,1,64]{2,1,0:T(1,128)}, u32[]{:S(2)}) %copy-start.4) | copy-done | bytes 280
  6.7 0.0 copy-start.5
  6.7 0.7 %copy-done.5 = s32[1,1,12]{2,1,0:T(1,128)S(1)} copy-done((s32[1,1,12]{2,1,0:T(1,128)S(1)}, s32[1,1,12]{2,1,0:T(1,128)}, u32[]{:S(2)}) %copy-start.5) | copy-done | bytes 72
  7.3 0.0 copy-start.6
  7.3 0.7 %copy-done.6 = s32[1,1,2]{2,1,0:T(1,128)S(1)} copy-done((s32[1,1,2]{2,1,0:T(1,128)S(1)}, s32[1,1,2]{2,1,0:T(1,128)}, u32[]{:S(2)}) %copy-start.6) | copy-done | bytes 32
  8.0 47.2 %galerkin.1 = (bf16[2,5,2,128,128]{4,3,2,1,0:T(8,128)(2,1)S(1)}, f32[2,3,2,128,128]{4,3,2,1,0:T(8,128)S(1)}) custom-call(bf16[64,128,128]{2,1,0:T(8,128)(2,1)S(1)} %bitcast.5, s32[1,1,64]{2,1,0:T(1,128)S(1)} %copy-done.3, s32[1,1,64]{2,1,0:T(1,128)S(1)} %copy-done.4, s32[1,1]{1,0:T(1,128)S(6)} %copy.13.fcount_hbm, bf16[12,128,128]{2,1,0:T(8,128)(2,1)S(1)} %bitcast.8, ...), custom_call_target="tpu_custom_call" | custom-call | tf_op jit(solution)/shard_map/galerkin/pallas_call | solution.py:427
  55.2 0.8 %copy.15 = bf16[1,1,2,5,2,128,128]{6,5,4,3,2,1,0:T(8,128)(2,1)} copy(bf16[1,1,2,5,2,128,128]{6,5,4,3,2,1,0:T(8,128)(2,1)S(1)} %bitcast.7) | data formatting | bytes 1310720
  56.1 0.9 %copy.16 = f32[1,2,3,2,128,128]{5,4,3,2,1,0:T(8,128)} copy(f32[1,2,3,2,128,128]{5,4,3,2,1,0:T(8,128)S(1)} %bitcast.6) | data formatting | bytes 1572864
Async XLA Ops:
  1.9 1.6 %copy-start = (bf16[1,1,64,128,128]{4,3,2,1,0:T(8,128)(2,1)S(1)}, bf16[1,1,64,128,128]{4,3,2,1,0:T(8,128)(2,1)}, u32[]{:S(2)}) copy-start(bf16[1,1,64,128,128]{4,3,2,1,0:T(8,128)(2,1)} %param.9) | copy-start | bytes 6291460
  3.5 1.0 %copy-start.1 = (bf16[1,1,12,128,128]{4,3,2,1,0:T(8,128)(2,1)S(1)}, bf16[1,1,12,128,128]{4,3,2,1,0:T(8,128)(2,1)}, u32[]{:S(2)}) copy-start(bf16[1,1,12,128,128]{4,3,2,1,0:T(8,128)(2,1)} %param.13) | copy-start | bytes 1179652
  4.5 0.8 %copy-start.2 = (bf16[1,1,2,128,128]{4,3,2,1,0:T(8,128)(2,1)S(1)}, bf16[1,1,2,128,128]{4,3,2,1,0:T(8,128)(2,1)}, u32[]{:S(2)}) copy-start(bf16[1,1,2,128,128]{4,3,2,1,0:T(8,128)(2,1)} %param.16) | copy-start | bytes 196612
  5.4 0.7 %copy-start.3 = (s32[1,1,64]{2,1,0:T(1,128)S(1)}, s32[1,1,64]{2,1,0:T(1,128)}, u32[]{:S(2)}) copy-start(s32[1,1,64]{2,1,0:T(1,128)} %rows_hbm.1) | copy-start | bytes 772
  6.0 0.7 %copy-start.4 = (s32[1,1,64]{2,1,0:T(1,128)S(1)}, s32[1,1,64]{2,1,0:T(1,128)}, u32[]{:S(2)}) copy-start(s32[1,1,64]{2,1,0:T(1,128)} %cols_hbm.1) | copy-start | bytes 772
  6.7 0.7 %copy-start.5 = (s32[1,1,12]{2,1,0:T(1,128)S(1)}, s32[1,1,12]{2,1,0:T(1,128)}, u32[]{:S(2)}) copy-start(s32[1,1,12]{2,1,0:T(1,128)} %codes_hbm.1) | copy-start | bytes 148
  7.3 0.7 %copy-start.6 = (s32[1,1,2]{2,1,0:T(1,128)S(1)}, s32[1,1,2]{2,1,0:T(1,128)}, u32[]{:S(2)}) copy-start(s32[1,1,2]{2,1,0:T(1,128)} %aggs_hbm.1) | copy-start | bytes 28

commit v2 on v1

--- a/solution.py
+++ b/solution.py
@@ -18,6 +18,7 @@
 BF = jnp.bfloat16
 F32 = jnp.float32
 MESH = pl.DeviceIdType.MESH
+VMEM_LIMIT = 62 << 20
 HALF = (BS, 2 * BS)
 REACH = (4, 3, 5, 2, 6, 1, 7)
 
@@ -27,17 +28,13 @@
 
 
 def kernel(
+    meta_hbm,
     a_hbm,
-    rows_hbm,
-    cols_hbm,
-    fcount_hbm,
     p_hbm,
-    codes_hbm,
-    pcount_hbm,
     l_hbm,
-    aggs_hbm,
-    one_ref,
-    two_ref,
+    one_hbm,
+    early_hbm,
+    late_hbm,
     a_buf,
     p_0,
     p_1,
@@ -45,22 +42,18 @@
     p_3,
     p_4,
     l_buf,
-    rows_s,
-    cols_v,
-    fcount_v,
-    codes_v,
-    pcount_v,
-    aggs_s,
+    meta_v,
+    meta_s,
     table_v,
     table_s,
     near_v,
     near_s,
     pt,
     run,
+    one_ref,
     wide,
     lifted,
     lifted_t,
-    c1,
     give_e,
     give_l,
     take_e,
@@ -82,6 +75,7 @@
     ag_recv,
     fw_send,
     fw_recv,
+    store_sem,
     reach_sem,
 ):
     p_bufs = (p_0, p_1, p_2, p_3, p_4)
@@ -96,20 +90,23 @@
 
     sources = ((0, -1), (0, 1), (-1, 0), (1, 0))
 
+    has = (None, col > 0, col < NC - 1, row > 0, row < NR - 1)
+    feeds = (None, has[2], has[1], has[4], has[3])
+
     barrier = pltpu.get_barrier_semaphore()
-    for dr, dc in sources:
-        pl.semaphore_signal(barrier, inc=1, device_id=at(dr, dc), device_id_type=MESH)
+    for (dr, dc), near in zip(sources, has[1:]):
+
+        @pl.when(near)
+        def _():
+            pl.semaphore_signal(barrier, inc=1, device_id=at(dr, dc), device_id_type=MESH)
+
 
     loads = [
-        pltpu.make_async_copy(cols_hbm, cols_v, load_sem.at[0]),
-        pltpu.make_async_copy(fcount_hbm, fcount_v, load_sem.at[1]),
-        pltpu.make_async_copy(codes_hbm, codes_v.at[0], load_sem.at[2]),
-        pltpu.make_async_copy(pcount_hbm, pcount_v.at[0], load_sem.at[3]),
-        pltpu.make_async_copy(aggs_hbm, aggs_s.at[0], load_sem.at[4]),
-        pltpu.make_async_copy(rows_hbm, rows_s, load_sem.at[5]),
-        pltpu.make_async_copy(p_hbm, p_0.at[pl.ds(0, NP)], load_sem.at[6]),
-        pltpu.make_async_copy(l_hbm, l_buf.at[0], load_sem.at[7]),
-        pltpu.make_async_copy(a_hbm, a_buf, load_sem.at[8]),
+        pltpu.make_async_copy(meta_hbm, meta_v.at[0], load_sem.at[0]),
+        pltpu.make_async_copy(meta_hbm, meta_s, load_sem.at[1]),
+        pltpu.make_async_copy(p_hbm, p_0.at[pl.ds(0, NP)], load_sem.at[2]),
+        pltpu.make_async_copy(l_hbm, l_buf.at[0], load_sem.at[3]),
+        pltpu.make_async_copy(a_hbm, a_buf, load_sem.at[4]),
     ]
     for load in loads:
         load.start()
@@ -117,13 +114,18 @@
         p_bufs[s][NP] = jnp.zeros((BS, BS), BF)
     run[NA] = jnp.zeros((W2, BS), F32)
 
-    pl.semaphore_wait(barrier, 4)
+    for s in range(1, 5):
+
+        @pl.when(jnp.logical_not(has[s]))
+        def _():
+            meta_v[s] = jnp.zeros((8, BS), jnp.int32)
+            l_buf[s] = jnp.zeros((CB, BS, BS), BF)
+
+    pl.semaphore_wait(barrier, sum(near.astype(jnp.int32) for near in has[1:]))
 
     def halo(s, item):
         src, dst = (
-            (codes_hbm, codes_v.at[s]),
-            (pcount_hbm, pcount_v.at[s]),
-            (aggs_hbm, aggs_s.at[s]),
+            (meta_hbm, meta_v.at[s]),
             (p_hbm, p_bufs[s].at[pl.ds(0, NP)]),
             (l_hbm, l_buf.at[s]),
         )[item]
@@ -138,55 +140,62 @@
         )
 
     order = (3, 4, 1, 2)
-    for items in ((0, 1, 2), (3,), (4,)):
-        for item in items:
-            for s in order:
+    for item in range(3):
+        for s in order:
+
+            @pl.when(feeds[s])
+            def _():
                 halo(s, item).start()
 
-    def widen(step, slot):
-        sem = reach_sem.at[slot]
+    def arrived(s, item):
+        @pl.when(has[s])
+        def _():
+            halo(s, item).wait_recv()
+
+
+    def spread(step, slot):
         for sign in (-1, 1):
-            pl.semaphore_signal(sem, inc=1, device_id=at(0, sign * step), device_id_type=MESH)
-        pl.semaphore_wait(sem, 2)
-
-    for load in loads[:4]:
-        load.wait()
+
+            @pl.when((col + sign * step >= 0) & (col + sign * step < NC))
+            def _():
+                pl.semaphore_signal(
+                    reach_sem.at[slot], inc=1, device_id=at(0, sign * step), device_id_type=MESH
+                )
+
+    def known(step, slot):
+        ends = (col >= step).astype(jnp.int32) + (col < NC - step).astype(jnp.int32)
+        pl.semaphore_wait(reach_sem.at[slot], ends)
+
+    spread(1, 0)
+
+    loads[0].wait()
     sub = lax.broadcasted_iota(jnp.int32, (BS, BS), 0)
     lane = lax.broadcasted_iota(jnp.int32, (BS, BS), 1)
 
     def down(vector, length):
-        wide_row = jnp.broadcast_to(vector, (length, length))
-        diag = sub[:length, :length] == lane[:length, :length]
-        return jnp.max(jnp.where(diag, wide_row, -1), axis=1, keepdims=True)
+        diag = sub[:length] == lane[:length]
+        return jnp.max(jnp.where(diag, vector, -1), axis=1, keepdims=True)
 
     def pick(match, length, missing):
         best = jnp.max(jnp.where(match, sub[:length], -1), axis=0, keepdims=True)
         return jnp.where(best < 0, missing, best)
 
-    cols = cols_v[...].reshape(1, NA)
+    cols = meta_v[0, 0:1]
     cols_down = down(cols, NA)
-    live = sub[:NA] < fcount_v[...]
-    cols_wide = jnp.concatenate([cols, cols], axis=1)
-    table_v[0:1] = pick(
-        (cols_down == cols_wide) & (sub[:NA] < lane[:NA]) & live, NA, NA
-    )
+    live = sub[:NA] < meta_v[0, 2:3]
+    table_v[0:1] = pick((cols_down == cols) & (sub[:NA] < lane[:NA]) & live, NA, NA)
     table_v[1:2] = pick((cols_down == lane[:NA]) & live, NA, NA)
 
     def place(s):
-        codes = codes_v[s].reshape(1, NP)
-        diag = sub[:16, :NP] == lane[:16, :NP]
-        codes_down = jnp.max(
-            jnp.where(diag, jnp.broadcast_to(codes, (16, NP)), -1), axis=1, keepdims=True
-        )
-        return pick((codes_down == lane[:16]) & (sub[:16] < pcount_v[s]), 16, NP)
+        codes_down = down(meta_v[s, 3:4], 16)
+        return pick((codes_down == lane[:16]) & (sub[:16] < meta_v[s, 4:5]), 16, NP)
 
     table_v[2:3] = place(0)
-    send_table = pltpu.make_async_copy(table_v, table_s, load_sem.at[9])
+    send_table = pltpu.make_async_copy(table_v, table_s, load_sem.at[5])
     send_table.start()
-    widen(1, 0)
     send_table.wait()
-    loads[5].wait()
-    loads[6].wait()
+    loads[1].wait()
+    loads[2].wait()
 
     def turn(i, carry):
         for coarse in range(CB):
@@ -195,16 +204,19 @@
         return carry
 
     lax.fori_loop(0, FB, turn, 0)
-    loads[8].wait()
+    known(1, 0)
+    spread(2, 1)
+    loads[4].wait()
 
     def slots(step, carry):
         for inner in range(4):
             k = step * 4 + inner
-            run[k] = dot(pt[rows_s[0, 0, k]], a_buf[k]) + run[table_s[0, k]]
+            run[k] = dot(pt[meta_s[1, k]], a_buf[k]) + run[table_s[0, k]]
         return carry
 
     lax.fori_loop(0, NA // 4, slots, 0)
-    widen(2, 1)
+    known(2, 1)
+    spread(4, 2)
 
     def widen_rows(s, carry):
         for m in range(FB):
@@ -213,31 +225,30 @@
         return carry
 
     lax.fori_loop(0, 5, widen_rows, 0)
-    widen(4, 2)
+    known(4, 2)
+    spread(8, 3)
 
     for s in range(1, 5):
-        for item in range(3):
-            halo(s, item).wait_recv()
+        arrived(s, 0)
+    near_v[0:1] = table_v[2:3]
+    near_v[8:9] = meta_v[0, 5:6]
     for s in range(1, 5):
         near_v[s : s + 1] = place(s)
-    near_v[0:1] = table_v[2:3]
-    send_near = pltpu.make_async_copy(near_v, near_s, load_sem.at[10])
+        near_v[8 + s : 9 + s] = meta_v[s, 5:6]
+    send_near = pltpu.make_async_copy(near_v, near_s, load_sem.at[6])
     send_near.start()
-    loads[4].wait()
-    loads[7].wait()
+    loads[3].wait()
 
     def lift(s):
         for j in range(CB):
             block = l_buf[s, j]
             for a in range(G2):
-                kept = jnp.where(aggs_s[s, 0, 0, j] == a, block, jnp.zeros_like(block))
+                kept = jnp.where(near_s[8 + s, j] == a, block, jnp.zeros_like(block))
                 lifted[s, pl.ds(j * BS, BS), pl.ds(a * BS, BS)] = kept
 
+    send_near.wait()
     lift(0)
     lifted_t[...] = lifted[0].T
-    send_near.wait()
-
-    inside = (None, col > 0, col < NC - 1, row > 0, row < NR - 1)
 
     def level_one(s):
         total = jnp.zeros((W2, W2), F32)
@@ -252,14 +263,13 @@
                 axis=0,
             )
             total += dot(wide[s, pair], right)
-        if inside[s] is not None:
-            total = jnp.where(inside[s], total, jnp.zeros_like(total))
         result = total.astype(BF)
         for coarse in range(CB):
             for j in range(CB):
                 one_ref[coarse, s, j] = result[
                     coarse * BS : (coarse + 1) * BS, j * BS : (j + 1) * BS
                 ]
+        leave(s).start()
         return result
 
     def half_term(firsts):
@@ -267,6 +277,9 @@
         for s, result in firsts:
             total += dot(result, lifted[s])
         return dot(lifted_t[...], total.astype(BF))
+
+    def leave(s):
+        return pltpu.make_async_copy(one_ref.at[:, s], one_hbm.at[:, s], store_sem.at[s])
 
     gives, takes, parts = (give_e, give_l), (take_e, take_l), (part_e, part_l)
     shares, whole = (rs_e, rs_l), (all_e, all_l)
@@ -361,46 +374,46 @@
 
     firsts = [(0, level_one(0))]
     for s in (1, 2):
-        halo(s, 3).wait_recv()
+        arrived(s, 1)
         firsts.append((s, level_one(s)))
     for s in (1, 2):
-        halo(s, 4).wait_recv()
+        arrived(s, 2)
         lift(s)
     early = half_term(firsts).astype(BF)
     for side in range(2):
         give_e[side] = early[side * BS : (side + 1) * BS]
     pair_copy(0).start()
+    known(8, 3)
     scatter(0)
 
+    terms = []
     for s in (3, 4):
-        halo(s, 3).wait_recv()
-        result = level_one(s)
-        halo(s, 4).wait_recv()
+        arrived(s, 1)
+        terms.append(dot(lifted_t[...], level_one(s)).astype(BF))
+    for s in (3, 4):
+        arrived(s, 2)
         lift(s)
-        give_l[s - 3] = half_term([(s, result)]).astype(BF)
+        give_l[s - 3] = dot(terms[s - 3], lifted[s]).astype(BF)
     pair_copy(1).start()
+    scatter(1)
     gather(0)
-    scatter(1)
+    gather(1)
     hand_over(0)
-    gather(1)
     hand_over(1)
+    leaving = [leave(s) for s in range(5)]
     for w in range(2):
         for dz in range(CHIPS):
             forward_arrival(w, dz).wait_recv()
-        size = HALF[w] // CHIPS
-        for side in range(2):
-            for piece in range(CHIPS):
-                block = whole[w][side, piece].astype(F32)
-                if w == 0:
-                    a, g, y = side, 0, piece * size
-                else:
-                    a, g, y = piece // 4, 1 + side, (piece % 4) * size
-                for b in range(G2):
-                    two_ref[a, g, b, pl.ds(y, size), :] = block[:, b * BS : (b + 1) * BS]
-
+        last = pltpu.make_async_copy(whole[w], (early_hbm, late_hbm)[w], store_sem.at[5 + w])
+        last.start()
+        leaving.append(last)
     for s in range(1, 5):
-        for item in range(5):
-            halo(s, item).wait_send()
+
+        @pl.when(feeds[s])
+        def _():
+            for item in range(3):
+                halo(s, item).wait_send()
+
     for w in range(2):
         pair_copy(w).wait_send()
         for dz in REACH:
@@ -408,6 +421,46 @@
             ag_copy(w, dz).wait_send()
         for dz in range(CHIPS):
             forward(w, dz).wait_send()
+    for copy in leaving:
+        copy.wait()
+
+
+def finish(one_in, early_in, late_in, one_out, two_out, one_v, early_v, late_v, two_v, take, give):
+    takes = [
+        pltpu.make_async_copy(src, dst, take.at[i])
+        for i, (src, dst) in enumerate(((early_in, early_v), (late_in, late_v), (one_in, one_v)))
+    ]
+    for copy in takes:
+        copy.start()
+    gives = []
+    for g in range(3):
+        if g < 2:
+            takes[g].wait()
+        for a in range(G2):
+            if g == 0:
+                rows = early_v[a].reshape(BS, W2)
+            else:
+                rows = late_v[g - 1, a * 4 : a * 4 + 4].reshape(BS, W2)
+            for b in range(G2):
+                two_v[a, g, b] = rows[:, b * BS : (b + 1) * BS].astype(F32)
+        gives.append(pltpu.make_async_copy(two_v.at[:, g], two_out.at[:, g], give.at[g]))
+        gives[-1].start()
+        if g == 1:
+            takes[2].wait()
+            gives.append(pltpu.make_async_copy(one_v, one_out, give.at[3]))
+            gives[-1].start()
+    for copy in gives:
+        copy.wait()
+
+
+def index_rows(*rows):
+    out = jnp.zeros((8, BS), jnp.int32)
+    for i, row in enumerate(rows):
+        if row.shape[1] > 1:
+            out += jnp.pad(row, ((i, 7 - i), (0, BS - row.shape[1])))
+    at = lax.broadcasted_iota(jnp.int32, (8, BS), 0)
+    out = jnp.where(at == 2, rows[2], out)
+    return jnp.where(at == 4, rows[4], out)
 
 
 def per_device(
@@ -422,37 +475,36 @@
     second_aggs,
 ):
     any_spec = pl.BlockSpec(memory_space=pl.ANY)
-    vmem = pl.BlockSpec(memory_space=pltpu.VMEM)
     dma = pltpu.SemaphoreType.DMA
-    one, two = pl.pallas_call(
+    meta = index_rows(
+        fine_cols[0], fine_rows[0], fine_counts, prolong_codes[0], prolong_counts, second_aggs[0]
+    )
+    one, early, late = pl.pallas_call(
         kernel,
         name="galerkin",
         out_shape=(
             jax.ShapeDtypeStruct((CB, 5, CB, BS, BS), BF),
-            jax.ShapeDtypeStruct((G2, 3, G2, BS, BS), F32),
+            jax.ShapeDtypeStruct((2, CHIPS, HALF[0] // CHIPS, W2), BF),
+            jax.ShapeDtypeStruct((2, CHIPS, HALF[1] // CHIPS, W2), BF),
         ),
-        in_specs=[any_spec] * 9,
-        out_specs=(vmem, vmem),
+        in_specs=[any_spec] * 4,
+        out_specs=(any_spec,) * 3,
         scratch_shapes=[
             pltpu.VMEM((NA, BS, BS), BF),
             *[pltpu.VMEM((NP + 1, BS, BS), BF)] * 5,
             pltpu.VMEM((5, CB, BS, BS), BF),
-            pltpu.SMEM((1, 1, NA), jnp.int32),
-            pltpu.VMEM((1, 1, NA), jnp.int32),
-            pltpu.VMEM((1, 1), jnp.int32),
-            pltpu.VMEM((5, 1, 1, NP), jnp.int32),
-            pltpu.VMEM((5, 1, 1), jnp.int32),
-            pltpu.SMEM((5, 1, 1, CB), jnp.int32),
-            pltpu.VMEM((8, BS), jnp.int32),
+            pltpu.VMEM((5, 8, BS), jnp.int32),
             pltpu.SMEM((8, BS), jnp.int32),
             pltpu.VMEM((8, BS), jnp.int32),
             pltpu.SMEM((8, BS), jnp.int32),
+            pltpu.VMEM((16, BS), jnp.int32),
+            pltpu.SMEM((16, BS), jnp.int32),
             pltpu.VMEM((FB, W2, BS), BF),
             pltpu.VMEM((NA + 1, W2, BS), F32),
+            pltpu.VMEM((CB, 5, CB, BS, BS), BF),
             pltpu.VMEM((5, FB // 2, W2, W2), BF),
             pltpu.VMEM((5, W2, W2), BF),
             pltpu.VMEM((W2, W2), BF),
-            pltpu.VMEM((8, BS), BF),
             pltpu.VMEM((2, HALF[0], W2), BF),
             pltpu.VMEM((2, HALF[1], W2), BF),
             pltpu.VMEM((HALF[0], W2), BF),
@@ -463,9 +515,9 @@
             pltpu.VMEM((CHIPS, HALF[1] // CHIPS, W2), BF),
             pltpu.VMEM((2, CHIPS, HALF[0] // CHIPS, W2), BF),
             pltpu.VMEM((2, CHIPS, HALF[1] // CHIPS, W2), BF),
-            dma((11,)),
-            dma((4, 5)),
-            dma((4, 5)),
+            dma((7,)),
+            dma((4, 3)),
+            dma((4, 3)),
             dma((2,)),
             dma((2,)),
             dma((2, CHIPS)),
@@ -474,22 +526,36 @@
             dma((2, CHIPS)),
             dma((2, CHIPS)),
             dma((2, CHIPS)),
-            pltpu.SemaphoreType.REGULAR((3,)),
+            dma((7,)),
+            pltpu.SemaphoreType.REGULAR((4,)),
         ],
         compiler_params=pltpu.CompilerParams(
-            collective_id=0, has_side_effects=True, vmem_limit_bytes=48 << 20
+            collective_id=0, has_side_effects=True, vmem_limit_bytes=VMEM_LIMIT
         ),
     )(
+        meta,
         fine_blocks[0, 0],
-        fine_rows,
-        fine_cols,
-        fine_counts,
         prolong_blocks[0, 0],
-        prolong_codes,
-        prolong_counts,
         second_blocks[0, 0],
-        second_aggs,
     )
+    one, two = pl.pallas_call(
+        finish,
+        name="finish",
+        out_shape=(
+            jax.ShapeDtypeStruct((CB, 5, CB, BS, BS), BF),
+            jax.ShapeDtypeStruct((G2, 3, G2, BS, BS), F32),
+        ),
+        in_specs=[any_spec] * 3,
+        out_specs=(any_spec,) * 2,
+        scratch_shapes=[
+            pltpu.VMEM((CB, 5, CB, BS, BS), BF),
+            pltpu.VMEM((2, CHIPS, HALF[0] // CHIPS, W2), BF),
+            pltpu.VMEM((2, CHIPS, HALF[1] // CHIPS, W2), BF),
+            pltpu.VMEM((G2, 3, G2, BS, BS), F32),
+            dma((3,)),
+            dma((4,)),
+        ],
+    )(one, early, late)
     return (one[None, None], two[None])
 
 

time: 57.2 us -> 45.4 us (0.79)
  the two profiles are of different devices: /device:TPU:1 before, /device:TPU:7 now
where the time goes in v2:
time: 45.4 us; the launch traced here: 45.2 us
  Pallas kernels  41.9 us (92%)
  between operations  1.94 us (4%)
  other arithmetic  1.38 us (3%)
    pallas_call x1, Pallas kernels, per_device(): pl.pallas_call(kernel, name='galerkin', out_shape=(jax.ShapeDtypeStruct((...  39.6 us
    pallas_call x1, Pallas kernels, per_device(): pl.pallas_call(finish, name='finish', out_shape=(jax.ShapeDtypeStruct((CB...  2.22 us
    select_n x1, other arithmetic, index_rows(): return jnp.where(at == 4, rows[4], out)  1.37 us

profile of v2, /device:TPU:7, one launch (start us, length us, event | category | flops | bytes accessed | tf_op | source)
XLA Modules:
  0.0 45.2 jit_solution(2920763002520220537)
XLA Ops:
  1.9 1.4 %select_select_fusion.meta_hbm = s32[8,128]{1,0:T(8,128)} fusion(s32[1,2]{1,0:T(1,128)} %bitcast.16, s32[1,12]{1,0:T(1,128)} %bitcast.17, s32[1,64]{1,0:T(1,128)} %bitcast.18, s32[1,64]{1,0:T(1,128)} %bitcast.19, s32[]{:T(128)} %bitcast.11, s32[]{:T(128)} %bitcast.12, pred[8]{0:T(512)(128)(4,1)S(1)} %get-tuple-element.12, pred[8]{0:T(512)(128)(4,1)S(1)} %get-tuple-element.13), kind=kLoop, calls=%fused_computation | loop fusion | flops 5120 | bytes 4688 | tf_op jit(solution)/shard_map/jit(_where)/select_n | solution.py:463
  3.3 39.6 %galerkin.1 = (bf16[2,5,2,128,128]{4,3,2,1,0:T(8,128)(2,1)}, bf16[2,8,16,256]{3,2,1,0:T(8,128)(2,1)}, bf16[2,8,32,256]{3,2,1,0:T(8,128)(2,1)}) custom-call(s32[8,128]{1,0:T(8,128)} %select_select_fusion.meta_hbm, bf16[64,128,128]{2,1,0:T(8,128)(2,1)} %bitcast.13, bf16[12,128,128]{2,1,0:T(8,128)(2,1)} %bitcast.14, bf16[2,128,128]{2,1,0:T(8,128)(2,1)} %bitcast.15), custom_call_target="tpu_custom_call" | custom-call | tf_op jit(solution)/shard_map/galerkin/pallas_call | solution.py:482
  42.9 2.2 %finish.1 = (bf16[2,5,2,128,128]{4,3,2,1,0:T(8,128)(2,1)}, f32[2,3,2,128,128]{4,3,2,1,0:T(8,128)}) custom-call(bf16[2,5,2,128,128]{4,3,2,1,0:T(8,128)(2,1)} %get-tuple-element.7.one_in, bf16[2,8,16,256]{3,2,1,0:T(8,128)(2,1)} %get-tuple-element.8.early_in, bf16[2,8,32,256]{3,2,1,0:T(8,128)(2,1)} %get-tuple-element.9.late_in), custom_call_target="tpu_custom_call" | custom-call | tf_op jit(solution)/shard_map/finish/pallas_call | solution.py:541
  (1 shorter events, 0.0 us)

commit v3 on v2

v3 whole, which is shorter than its diff:
```python
import jax
import jax.numpy as jnp
from jax import lax
from jax.experimental import pallas as pl
from jax.experimental.pallas import tpu as pltpu
from jax.sharding import PartitionSpec as P

BS = 128
FB = 8
CB = 2
NA = 64
NP = 12
G2 = 2
NR = 32
NC = 16
CHIPS = NC // 2
W2 = CB * BS
BF = jnp.bfloat16
F32 = jnp.float32
MESH = pl.DeviceIdType.MESH
VMEM_LIMIT = 67043328 - (1088 << 10)
HALF = (BS, 2 * BS)
REACH = (4, 3, 5, 2, 6, 1, 7)
GROUPS = ((1, 7, 2, 6), (3, 5), (4,))


def dot(a, b):
    return jnp.dot(a, b, preferred_element_type=F32)


def kernel(
    cols_hbm,
    rows_hbm,
    fcount_s,
    codes_hbm,
    pcount_s,
    aggs_hbm,
    a_hbm,
    p_hbm,
    l_hbm,
    one_ref,
    all_e,
    all_l,
    a_buf,
    p_0,
    p_1,
    p_2,
    p_3,
    p_4,
    l_buf,
    meta_v,
    cols_v,
    codes_v,
    aggs_v,
    rows_s,
    table_v,
    table_s,
    near_v,
    near_s,
    pt,
    run,
    wide,
    lifted,
    lifted_t,
    give_e,
    give_l,
    take_e,
    take_l,
    part_e,
    part_l,
    rs_e,
    rs_l,
    load_sem,
    halo_send,
    halo_recv,
    pair_send,
    pair_recv,
    rs_send,
    rs_recv,
    ag_send,
    ag_recv,
    fw_send,
    fw_recv,
    reach_sem,
):
    p_bufs = (p_0, p_1, p_2, p_3, p_4)
    row = lax.axis_index("row")
    col = lax.axis_index("col")
    chip = col // 2
    core = col % 2
    partner = 2 * chip + 1 - core

    def at(dr, dc):
        return {"row": (row + dr + NR) % NR, "col": (col + dc + NC) % NC}

    sources = ((0, -1), (0, 1), (-1, 0), (1, 0))

    has = (None, col > 0, col < NC - 1, row > 0, row < NR - 1)
    feeds = (None, has[2], has[1], has[4], has[3])

    barrier = pltpu.get_barrier_semaphore()
    for (dr, dc), near in zip(sources, has[1:]):

        @pl.when(near)
        def _():
            pl.semaphore_signal(barrier, inc=1, device_id=at(dr, dc), device_id_type=MESH)


    loads = [
        pltpu.make_async_copy(codes_hbm, codes_v, load_sem.at[0]),
        pltpu.make_async_copy(aggs_hbm, aggs_v, load_sem.at[1]),
        pltpu.make_async_copy(cols_hbm, cols_v, load_sem.at[2]),
        pltpu.make_async_copy(rows_hbm, rows_s, load_sem.at[3]),
        pltpu.make_async_copy(p_hbm, p_0.at[pl.ds(0, NP)], load_sem.at[4]),
        pltpu.make_async_copy(l_hbm, l_buf.at[0], load_sem.at[5]),
        pltpu.make_async_copy(a_hbm, a_buf, load_sem.at[6]),
    ]
    for load in loads:
        load.start()
    for s in range(5):
        p_bufs[s][NP] = jnp.zeros((BS, BS), BF)
    run[NA] = jnp.zeros((W2, BS), F32)

    for s in range(1, 5):

        @pl.when(jnp.logical_not(has[s]))
        def _():
            meta_v[s] = jnp.zeros((8, BS), jnp.int32)
            l_buf[s] = jnp.zeros((CB, BS, BS), BF)

    meta_v[0] = jnp.zeros((8, BS), jnp.int32)
    meta_v[0, 1:2] = jnp.full((1, BS), pcount_s[0, 0], jnp.int32)
    loads[0].wait()
    meta_v[0, 0:1, 0:NP] = codes_v[0]
    loads[1].wait()
    meta_v[0, 2:3, 0:CB] = aggs_v[0]

    pl.semaphore_wait(barrier, sum(near.astype(jnp.int32) for near in has[1:]))

    def halo(s, item):
        src, dst = (
            (meta_v.at[0], meta_v.at[s]),
            (p_hbm, p_bufs[s].at[pl.ds(0, NP)]),
            (l_hbm, l_buf.at[s]),
        )[item]
        dr, dc = sources[s - 1]
        return pltpu.make_async_remote_copy(
            src_ref=src,
            dst_ref=dst,
            send_sem=halo_send.at[s - 1, min(item, 1)],
            recv_sem=halo_recv.at[s - 1, item],
            device_id=at(-dr, -dc),
            device_id_type=MESH,
        )

    order = (3, 4, 1, 2)
    for item in range(3):
        for s in order:

            @pl.when(feeds[s])
            def _():
                halo(s, item).start()

    def arrived(s, item):
        @pl.when(has[s])
        def _():
            halo(s, item).wait_recv()


    def spread(step, slot):
        for sign in (-1, 1):

            @pl.when((col + sign * step >= 0) & (col + sign * step < NC))
            def _():
                pl.semaphore_signal(
                    reach_sem.at[slot], inc=1, device_id=at(0, sign * step), device_id_type=MESH
                )

    def known(step, slot):
        ends = (col >= step).astype(jnp.int32) + (col < NC - step).astype(jnp.int32)
        pl.semaphore_wait(reach_sem.at[slot], ends)

    spread(1, 0)

    sub = lax.broadcasted_iota(jnp.int32, (BS, BS), 0)
    lane = lax.broadcasted_iota(jnp.int32, (BS, BS), 1)

    def down(vector, length):
        diag = sub[:length] == lane[:length]
        return jnp.max(jnp.where(diag, vector, -1), axis=1, keepdims=True)

    def pick(match, length, missing):
        best = jnp.max(jnp.where(match, sub[:length], -1), axis=0, keepdims=True)
        return jnp.where(best < 0, missing, best)

    def place(s):
        codes_down = down(meta_v[s, 0:1], 16)
        return pick((codes_down == lane[:16]) & (sub[:16] < meta_v[s, 1:2]), 16, NP)

    loads[2].wait()
    cols = jnp.concatenate([cols_v[0], cols_v[0]], axis=1)
    cols_down = down(cols, NA)
    live = sub[:NA] < fcount_s[0, 0]
    table_v[0:1] = pick((cols_down == cols) & (sub[:NA] < lane[:NA]) & live, NA, NA)
    table_v[1:2] = pick((cols_down == lane[:NA]) & live, NA, NA)
    table_v[2:3] = place(0)
    send_table = pltpu.make_async_copy(table_v, table_s, load_sem.at[7])
    send_table.start()
    loads[4].wait()
    for slot in range(NP + 1):
        pt[slot] = p_0[slot].T
    loads[3].wait()
    send_table.wait()
    known(1, 0)
    spread(2, 1)
    loads[6].wait()

    def slots(step, carry):
        for inner in range(4):
            k = step * 4 + inner
            i = rows_s[0, 0, k]
            own = jnp.concatenate([pt[table_s[2, i * CB + j]] for j in range(CB)], axis=0)
            run[k] = dot(own, a_buf[k]) + run[table_s[0, k]]
        return carry

    lax.fori_loop(0, 12, slots, 0)
    known(2, 1)
    spread(4, 2)
    for s in range(1, 5):
        arrived(s, 0)
    near_v[0:1] = table_v[2:3]
    near_v[8:9] = meta_v[0, 2:3]
    for s in range(1, 5):
        near_v[s : s + 1] = place(s)
        near_v[8 + s : 9 + s] = meta_v[s, 2:3]
    send_near = pltpu.make_async_copy(near_v, near_s, load_sem.at[8])
    send_near.start()
    lax.fori_loop(12, NA // 4, slots, 0)
    known(4, 2)
    spread(8, 3)

    def widen_rows(s, carry):
        for m in range(FB):
            slot = table_s[1, s * FB + m]
            wide[s, m // 2, :, pl.ds((m % 2) * BS, BS)] = run[slot].astype(BF)
        return carry

    lax.fori_loop(0, 5, widen_rows, 0)
    loads[5].wait()
    send_near.wait()

    def lift(s):
        for j in range(CB):
            block = l_buf[s, j]
            for a in range(G2):
                kept = jnp.where(near_s[8 + s, j] == a, block, jnp.zeros_like(block))
                lifted[s, pl.ds(j * BS, BS), pl.ds(a * BS, BS)] = kept

    lift(0)
    lifted_t[...] = lifted[0].T

    def level_one(s):
        total = jnp.zeros((W2, W2), F32)
        for pair in range(FB // 2):
            right = jnp.concatenate(
                [
                    jnp.concatenate(
                        [p_bufs[s][near_s[s, (2 * pair + low) * CB + j]] for j in range(CB)], axis=1
                    )
                    for low in range(2)
                ],
                axis=0,
            )
            total += dot(wide[s, pair], right)
        result = total.astype(BF)
        for coarse in range(CB):
            for j in range(CB):
                one_ref[coarse, s, j] = result[
                    coarse * BS : (coarse + 1) * BS, j * BS : (j + 1) * BS
                ]
        return result

    def half_term(firsts):
        total = jnp.zeros((W2, W2), F32)
        for s, result in firsts:
            total += dot(result, lifted[s])
        return dot(lifted_t[...], total.astype(BF))

    gives, takes, parts = (give_e, give_l), (take_e, take_l), (part_e, part_l)
    shares, whole = (rs_e, rs_l), (all_e, all_l)

    def pair_copy(w):
        return pltpu.make_async_remote_copy(
            src_ref=gives[w].at[1 - core],
            dst_ref=takes[w],
            send_sem=pair_send.at[w],
            recv_sem=pair_recv.at[w],
            device_id={"row": row, "col": partner},
            device_id_type=MESH,
        )

    def peer(dz):
        return {"row": row, "col": 2 * ((chip + dz) % CHIPS) + core}

    def rs_copy(w, dz):
        return pltpu.make_async_remote_copy(
            src_ref=parts[w].at[(chip + dz) % CHIPS],
            dst_ref=shares[w].at[dz - 1],
            send_sem=rs_send.at[w],
            recv_sem=rs_recv.at[w],
            device_id=peer(dz),
            device_id_type=MESH,
        )

    def together(ref, count, send_sem, recv_sem):
        part = ref.at[pl.ds(0, count)]
        return pltpu.make_async_remote_copy(
            src_ref=part,
            dst_ref=part,
            send_sem=send_sem,
            recv_sem=recv_sem,
            device_id=peer(1),
            device_id_type=MESH,
        )

    def ag_copy(w, dz, group):
        return pltpu.make_async_remote_copy(
            src_ref=whole[w].at[core, chip],
            dst_ref=whole[w].at[core, chip],
            send_sem=ag_send.at[w],
            recv_sem=ag_recv.at[w, group],
            device_id=peer(dz),
            device_id_type=MESH,
        )

    def forward(w, dz):
        piece = whole[w].at[core, (chip - dz + CHIPS) % CHIPS]
        return pltpu.make_async_remote_copy(
            src_ref=piece,
            dst_ref=piece,
            send_sem=fw_send.at[w],
            recv_sem=fw_recv.at[w],
            device_id={"row": row, "col": partner},
            device_id_type=MESH,
        )

    def scatter(w):
        pair_copy(w).wait_recv()
        total = gives[w][core].astype(F32) + takes[w][...].astype(F32)
        parts[w][...] = total.astype(BF).reshape(CHIPS, HALF[w] // CHIPS, W2)
        for dz in REACH:
            rs_copy(w, dz).start()

    def gather(w):
        together(shares[w], CHIPS - 1, rs_send.at[w], rs_recv.at[w]).wait_recv()
        total = parts[w][chip].astype(F32)
        for dz in range(1, CHIPS):
            total += shares[w][dz - 1].astype(F32)
        whole[w][core, chip] = total.astype(BF)
        for group in (2, 1, 0):
            for dz in GROUPS[group]:
                ag_copy(w, dz, group).start()
        forward(w, 0).start()

    def hand_over(w, group):
        count = len(GROUPS[group])
        together(whole[w].at[core], count, ag_send.at[w], ag_recv.at[w, group]).wait_recv()
        for dz in GROUPS[group]:
            forward(w, dz).start()

    firsts = [(0, level_one(0))]
    for s in (1, 2):
        arrived(s, 1)
        firsts.append((s, level_one(s)))
    for s in (1, 2):
        arrived(s, 2)
        lift(s)
    early = half_term(firsts).astype(BF)
    for side in range(2):
        give_e[side] = early[side * BS : (side + 1) * BS]
    pair_copy(0).start()
    known(8, 3)
    scatter(0)

    terms = []
    for s in (3, 4):
        arrived(s, 1)
        terms.append(dot(lifted_t[...], level_one(s)).astype(BF))
    for s in (3, 4):
        arrived(s, 2)
        lift(s)
        give_l[s - 3] = dot(terms[s - 3], lifted[s]).astype(BF)
    pair_copy(1).start()
    scatter(1)
    gather(0)
    gather(1)
    for group in range(3):
        hand_over(0, group)
    for group in range(3):
        hand_over(1, group)
    for s in range(1, 5):

        @pl.when(feeds[s])
        def _():
            halo(s, 0).wait_send()
            together(a_buf, NP + CB, halo_send.at[s - 1, 1], halo_recv.at[s - 1, 1]).wait_send()

    for w in range(2):
        pair_copy(w).wait_send()
        together(parts[w], CHIPS - 1, rs_send.at[w], rs_recv.at[w]).wait_send()
        together(whole[w].at[core], CHIPS - 1, ag_send.at[w], ag_recv.at[w, 0]).wait_send()
        together(whole[w].at[core], CHIPS, fw_send.at[w], fw_recv.at[w]).wait_send()
    for w in range(2):
        together(whole[w].at[1 - core], CHIPS, fw_send.at[w], fw_recv.at[w]).wait_recv()


def finish(one_v, early_v, late_v, one_out, two_out, two_v, give):
    gives = [pltpu.make_async_copy(one_v, one_out, give.at[3])]
    gives[0].start()
    for g in range(3):
        for a in range(G2):
            if g == 0:
                rows = early_v[a].reshape(BS, W2)
            else:
                rows = late_v[g - 1, a * 4 : a * 4 + 4].reshape(BS, W2)
            for b in range(G2):
                two_v[a, g, b] = rows[:, b * BS : (b + 1) * BS].astype(F32)
        gives.append(pltpu.make_async_copy(two_v.at[:, g], two_out.at[:, g], give.at[g]))
        gives[-1].start()
    for copy in gives:
        copy.wait()


def per_device(
    fine_blocks,
    fine_rows,
    fine_cols,
    fine_counts,
    prolong_blocks,
    prolong_codes,
    prolong_counts,
    second_blocks,
    second_aggs,
):
    any_spec = pl.BlockSpec(memory_space=pl.ANY)
    vmem = pl.BlockSpec(memory_space=pltpu.VMEM)
    smem = pl.BlockSpec(memory_space=pltpu.SMEM)
    dma = pltpu.SemaphoreType.DMA
    one, early, late = pl.pallas_call(
        kernel,
        name="galerkin",
        out_shape=(
            pltpu.VMEM((CB, 5, CB, BS, BS), BF),
            pltpu.VMEM((2, CHIPS, HALF[0] // CHIPS, W2), BF),
            pltpu.VMEM((2, CHIPS, HALF[1] // CHIPS, W2), BF),
        ),
        in_specs=[any_spec] * 2 + [smem, any_spec] * 2 + [any_spec] * 3,
        out_specs=(vmem,) * 3,
        scratch_shapes=[
            pltpu.VMEM((NA, BS, BS), BF),
            *[pltpu.VMEM((NP + 1, BS, BS), BF)] * 5,
            pltpu.VMEM((5, CB, BS, BS), BF),
            pltpu.VMEM((5, 8, BS), jnp.int32),
            pltpu.VMEM((1, 1, NA), jnp.int32),
            pltpu.VMEM((1, 1, NP), jnp.int32),
            pltpu.VMEM((1, 1, CB), jnp.int32),
            pltpu.SMEM((1, 1, NA), jnp.int32),
            pltpu.VMEM((8, BS), jnp.int32),
            pltpu.SMEM((8, BS), jnp.int32),
            pltpu.VMEM((16, BS), jnp.int32),
            pltpu.SMEM((16, BS), jnp.int32),
            pltpu.VMEM((NP + 1, BS, BS), BF),
            pltpu.VMEM((NA + 1, W2, BS), F32),
            pltpu.VMEM((5, FB // 2, W2, W2), BF),
            pltpu.VMEM((5, W2, W2), BF),
            pltpu.VMEM((W2, W2), BF),
            pltpu.VMEM((2, HALF[0], W2), BF),
            pltpu.VMEM((2, HALF[1], W2), BF),
            pltpu.VMEM((HALF[0], W2), BF),
            pltpu.VMEM((HALF[1], W2), BF),
            pltpu.VMEM((CHIPS, HALF[0] // CHIPS, W2), BF),
            pltpu.VMEM((CHIPS, HALF[1] // CHIPS, W2), BF),
            pltpu.VMEM((CHIPS - 1, HALF[0] // CHIPS, W2), BF),
            pltpu.VMEM((CHIPS - 1, HALF[1] // CHIPS, W2), BF),
            dma((9,)),
            dma((4, 2)),
            dma((4, 3)),
            dma((2,)),
            dma((2,)),
            dma((2,)),
            dma((2,)),
            dma((2,)),
            dma((2, 3)),
            dma((2,)),
            dma((2,)),
            pltpu.SemaphoreType.REGULAR((4,)),
        ],
        compiler_params=pltpu.CompilerParams(
            collective_id=0, has_side_effects=True, vmem_limit_bytes=VMEM_LIMIT
        ),
    )(
        fine_cols,
        fine_rows,
        fine_counts,
        prolong_codes,
        prolong_counts,
        second_aggs,
        fine_blocks[0, 0],
        prolong_blocks[0, 0],
        second_blocks[0, 0],
    )
    one, two = pl.pallas_call(
        finish,
        name="finish",
        out_shape=(
            jax.ShapeDtypeStruct((CB, 5, CB, BS, BS), BF),
            jax.ShapeDtypeStruct((G2, 3, G2, BS, BS), F32),
        ),
        in_specs=[vmem] * 3,
        out_specs=(any_spec,) * 2,
        scratch_shapes=[pltpu.VMEM((G2, 3, G2, BS, BS), F32), dma((4,))],
    )(*(pltpu.with_memory_space_constraint(x, pltpu.VMEM) for x in (one, early, late)))
    return (one[None, None], two[None])


def solution(mesh):
    in_specs = (
        P("row", "col", None, None, None),
        P("row", "col", None),
        P("row", "col", None),
        P("row", "col"),
        P("row", "col", None, None, None),
        P("row", "col", None),
        P("row", "col"),
        P("row", "col", None, None, None),
        P("row", "col", None),
    )
    out_specs = (
        P("row", "col", None, None, None, None, None),
        P("row", None, None, None, None, None),
    )
    return jax.shard_map(
        per_device, mesh=mesh, in_specs=in_specs, out_specs=out_specs, check_vma=False
    )
```

time: 45.4 us -> 41.2 us (0.907)
  Pallas kernels: 41.9 us -> 39.2 us
  other arithmetic: 1.38 us -> 0 us
    pallas_call x1, Pallas kernels: 39.6 us -> 38 us  [per_device(): pl.pallas_call(kernel, name='galerkin', out_shape=(pltpu.VMEM((CB, 5, CB,...]
    select_n x1 -> x0, other arithmetic: 1.37 us -> none  [index_rows(): return jnp.where(at == 4, rows[4], out)]
    pallas_call x1, Pallas kernels: 2.22 us -> 1.13 us  [per_device(): pl.pallas_call(finish, name='finish', out_shape=(jax.ShapeDtypeStruct((CB...]
where the time goes in v3:
time: 41.2 us; the launch traced here: 41.1 us
  Pallas kernels  39.2 us (95%)
  between operations  1.93 us (5%)
    pallas_call x1, Pallas kernels, per_device(): pl.pallas_call(kernel, name='galerkin', out_shape=(pltpu.VMEM((CB, 5, CB,...  38 us
    pallas_call x1, Pallas kernels, per_device(): pl.pallas_call(finish, name='finish', out_shape=(jax.ShapeDtypeStruct((CB...  1.13 us

profile of v3, /device:TPU:7, one launch (start us, length us, event | category | flops | bytes accessed | tf_op | source)
XLA Modules:
  0.0 41.1 jit_solution(15629720125937036840)
XLA Ops:
  1.9 38.0 %galerkin.1 = (bf16[2,5,2,128,128]{4,3,2,1,0:T(8,128)(2,1)S(1)}, bf16[2,8,16,256]{3,2,1,0:T(8,128)(2,1)S(1)}, bf16[2,8,32,256]{3,2,1,0:T(8,128)(2,1)S(1)}) custom-call(s32[1,1,64]{2,1,0:T(1,128)} %cols_hbm.1, s32[1,1,64]{2,1,0:T(1,128)} %rows_hbm.1, s32[1,1]{1,0:T(1,128)S(6)} %copy.11.fcount_s, s32[1,1,12]{2,1,0:T(1,128)} %codes_hbm.1, ...), custom_call_target="tpu_custom_call" | custom-call | tf_op jit(solution)/shard_map/galerkin/pallas_call | solution.py:449
  40.0 1.1 %finish.1 = (bf16[2,5,2,128,128]{4,3,2,1,0:T(8,128)(2,1)}, f32[2,3,2,128,128]{4,3,2,1,0:T(8,128)}) custom-call(bf16[2,5,2,128,128]{4,3,2,1,0:T(8,128)(2,1)S(1)} %get-tuple-element.7.one_v, bf16[2,8,16,256]{3,2,1,0:T(8,128)(2,1)S(1)} %get-tuple-element.8.early_v, bf16[2,8,32,256]{3,2,1,0:T(8,128)(2,1)S(1)} %get-tuple-element.9.late_v), custom_call_target="tpu_custom_call" | custom-call | tf_op jit(solution)/shard_map/finish/pallas_call | solution.py:512

commit v4 on v3

--- a/solution.py
+++ b/solution.py
@@ -45,8 +45,7 @@
     p_0,
     p_1,
     p_2,
-    p_3,
-    p_4,
+    p_row,
     l_buf,
     meta_v,
     cols_v,
@@ -60,6 +59,7 @@
     pt,
     run,
     wide,
+    folded,
     lifted,
     lifted_t,
     give_e,
@@ -83,7 +83,7 @@
     fw_recv,
     reach_sem,
 ):
-    p_bufs = (p_0, p_1, p_2, p_3, p_4)
+    p_bufs = (p_0, p_1, p_2, p_row.at[0], p_row.at[1])
     row = lax.axis_index("row")
     col = lax.axis_index("col")
     chip = col // 2
@@ -140,8 +140,8 @@
     def halo(s, item):
         src, dst = (
             (meta_v.at[0], meta_v.at[s]),
-            (p_hbm, p_bufs[s].at[pl.ds(0, NP)]),
-            (l_hbm, l_buf.at[s]),
+            (p_0.at[pl.ds(0, NP)], p_bufs[s].at[pl.ds(0, NP)]),
+            (l_buf.at[0], l_buf.at[s]),
         )[item]
         dr, dc = sources[s - 1]
         return pltpu.make_async_remote_copy(
@@ -153,6 +153,8 @@
             device_id_type=MESH,
         )
 
+    loads[4].wait()
+    loads[5].wait()
     order = (3, 4, 1, 2)
     for item in range(3):
         for s in order:
@@ -206,7 +208,6 @@
     table_v[2:3] = place(0)
     send_table = pltpu.make_async_copy(table_v, table_s, load_sem.at[7])
     send_table.start()
-    loads[4].wait()
     for slot in range(NP + 1):
         pt[slot] = p_0[slot].T
     loads[3].wait()
@@ -223,9 +224,12 @@
             run[k] = dot(own, a_buf[k]) + run[table_s[0, k]]
         return carry
 
-    lax.fori_loop(0, 12, slots, 0)
+    lax.fori_loop(0, 4, slots, 0)
     known(2, 1)
     spread(4, 2)
+    lax.fori_loop(4, 12, slots, 0)
+    known(4, 2)
+    spread(8, 3)
     for s in range(1, 5):
         arrived(s, 0)
     near_v[0:1] = table_v[2:3]
@@ -236,8 +240,6 @@
     send_near = pltpu.make_async_copy(near_v, near_s, load_sem.at[8])
     send_near.start()
     lax.fori_loop(12, NA // 4, slots, 0)
-    known(4, 2)
-    spread(8, 3)
 
     def widen_rows(s, carry):
         for m in range(FB):
@@ -246,7 +248,6 @@
         return carry
 
     lax.fori_loop(0, 5, widen_rows, 0)
-    loads[5].wait()
     send_near.wait()
 
     def lift(s):
@@ -259,19 +260,21 @@
     lift(0)
     lifted_t[...] = lifted[0].T
 
+    def dense(block, s, pair):
+        return jnp.concatenate(
+            [
+                jnp.concatenate(
+                    [block(near_s[s, (2 * pair + low) * CB + j]) for j in range(CB)], axis=1
+                )
+                for low in range(2)
+            ],
+            axis=0,
+        )
+
     def level_one(s):
         total = jnp.zeros((W2, W2), F32)
         for pair in range(FB // 2):
-            right = jnp.concatenate(
-                [
-                    jnp.concatenate(
-                        [p_bufs[s][near_s[s, (2 * pair + low) * CB + j]] for j in range(CB)], axis=1
-                    )
-                    for low in range(2)
-                ],
-                axis=0,
-            )
-            total += dot(wide[s, pair], right)
+            total += dot(wide[s, pair], dense(lambda slot: p_bufs[s][slot], s, pair))
         result = total.astype(BF)
         for coarse in range(CB):
             for j in range(CB):
@@ -280,18 +283,24 @@
                 ]
         return result
 
+    def late_half(d):
+        total = jnp.zeros((W2, W2), F32)
+        for pair in range(FB // 2):
+            total += dot(folded[d, pair], dense(lambda slot: p_row[d, slot], 3 + d, pair))
+        return total.astype(BF)
+
     def half_term(firsts):
         total = jnp.zeros((W2, W2), F32)
         for s, result in firsts:
             total += dot(result, lifted[s])
         return dot(lifted_t[...], total.astype(BF))
 
-    gives, takes, parts = (give_e, give_l), (take_e, take_l), (part_e, part_l)
+    takes, parts = (take_e, take_l), (part_e, part_l)
     shares, whole = (rs_e, rs_l), (all_e, all_l)
 
     def pair_copy(w):
         return pltpu.make_async_remote_copy(
-            src_ref=gives[w].at[1 - core],
+            src_ref=give_l if w else give_e.at[1 - core],
             dst_ref=takes[w],
             send_sem=pair_send.at[w],
             recv_sem=pair_recv.at[w],
@@ -344,9 +353,9 @@
             device_id_type=MESH,
         )
 
-    def scatter(w):
+    def scatter(w, own):
         pair_copy(w).wait_recv()
-        total = gives[w][core].astype(F32) + takes[w][...].astype(F32)
+        total = own + takes[w][...].astype(F32)
         parts[w][...] = total.astype(BF).reshape(CHIPS, HALF[w] // CHIPS, W2)
         for dz in REACH:
             rs_copy(w, dz).start()
@@ -380,19 +389,24 @@
         give_e[side] = early[side * BS : (side + 1) * BS]
     pair_copy(0).start()
     known(8, 3)
-    scatter(0)
-
-    terms = []
+    scatter(0, give_e[core].astype(F32))
+
+    for d in range(2):
+        for pair in range(FB // 2):
+            folded[d, pair] = dot(lifted_t[...], wide[3 + d, pair]).astype(BF)
     for s in (3, 4):
         arrived(s, 1)
-        terms.append(dot(lifted_t[...], level_one(s)).astype(BF))
+    away, kept = late_half(1 - core), late_half(core)
     for s in (3, 4):
         arrived(s, 2)
         lift(s)
-        give_l[s - 3] = dot(terms[s - 3], lifted[s]).astype(BF)
+    give_l[...] = dot(away, lifted[4 - core]).astype(BF)
     pair_copy(1).start()
-    scatter(1)
+    own = dot(kept, lifted[3 + core])
+    scatter(1, own)
     gather(0)
+    for s in (3, 4):
+        level_one(s)
     gather(1)
     for group in range(3):
         hand_over(0, group)
@@ -458,7 +472,8 @@
         out_specs=(vmem,) * 3,
         scratch_shapes=[
             pltpu.VMEM((NA, BS, BS), BF),
-            *[pltpu.VMEM((NP + 1, BS, BS), BF)] * 5,
+            *[pltpu.VMEM((NP + 1, BS, BS), BF)] * 3,
+            pltpu.VMEM((2, NP + 1, BS, BS), BF),
             pltpu.VMEM((5, CB, BS, BS), BF),
             pltpu.VMEM((5, 8, BS), jnp.int32),
             pltpu.VMEM((1, 1, NA), jnp.int32),
@@ -472,10 +487,11 @@
             pltpu.VMEM((NP + 1, BS, BS), BF),
             pltpu.VMEM((NA + 1, W2, BS), F32),
             pltpu.VMEM((5, FB // 2, W2, W2), BF),
+            pltpu.VMEM((2, FB // 2, W2, W2), BF),
             pltpu.VMEM((5, W2, W2), BF),
             pltpu.VMEM((W2, W2), BF),
             pltpu.VMEM((2, HALF[0], W2), BF),
-            pltpu.VMEM((2, HALF[1], W2), BF),
+            pltpu.VMEM((HALF[1], W2), BF),
             pltpu.VMEM((HALF[0], W2), BF),
             pltpu.VMEM((HALF[1], W2), BF),
             pltpu.VMEM((CHIPS, HALF[0] // CHIPS, W2), BF),

time: 41.2 us -> 40.7 us (0.988)
  Pallas kernels: 39.2 us -> 38.3 us
    pallas_call x1, Pallas kernels: 38 us -> 37.2 us  [per_device(): pl.pallas_call(kernel, name='galerkin', out_shape=(pltpu.VMEM((CB, 5, CB,...]
where the time goes in v4:
time: 40.7 us; the launch traced here: 40.2 us
  Pallas kernels  38.3 us (94%)
  between operations  1.93 us (5%)
    pallas_call x1, Pallas kernels, per_device(): pl.pallas_call(kernel, name='galerkin', out_shape=(pltpu.VMEM((CB, 5, CB,...  37.2 us
    pallas_call x1, Pallas kernels, per_device(): pl.pallas_call(finish, name='finish', out_shape=(jax.ShapeDtypeStruct((CB...  1.13 us

profile of v4, /device:TPU:7, one launch (start us, length us, event | category | flops | bytes accessed | tf_op | source)
XLA Modules:
  0.0 40.2 jit_solution(12998435249907910318)
XLA Ops:
  1.9 37.2 %galerkin.1 = (bf16[2,5,2,128,128]{4,3,2,1,0:T(8,128)(2,1)S(1)}, bf16[2,8,16,256]{3,2,1,0:T(8,128)(2,1)S(1)}, bf16[2,8,32,256]{3,2,1,0:T(8,128)(2,1)S(1)}) custom-call(s32[1,1,64]{2,1,0:T(1,128)} %cols_hbm.1, s32[1,1,64]{2,1,0:T(1,128)} %rows_hbm.1, s32[1,1]{1,0:T(1,128)S(6)} %copy.11.fcount_s, s32[1,1,12]{2,1,0:T(1,128)} %codes_hbm.1, ...), custom_call_target="tpu_custom_call" | custom-call | tf_op jit(solution)/shard_map/galerkin/pallas_call | solution.py:463
  39.1 1.1 %finish.1 = (bf16[2,5,2,128,128]{4,3,2,1,0:T(8,128)(2,1)}, f32[2,3,2,128,128]{4,3,2,1,0:T(8,128)}) custom-call(bf16[2,5,2,128,128]{4,3,2,1,0:T(8,128)(2,1)S(1)} %get-tuple-element.7.one_v, bf16[2,8,16,256]{3,2,1,0:T(8,128)(2,1)S(1)} %get-tuple-element.8.early_v, bf16[2,8,32,256]{3,2,1,0:T(8,128)(2,1)S(1)} %get-tuple-element.9.late_v), custom_call_target="tpu_custom_call" | custom-call | tf_op jit(solution)/shard_map/finish/pallas_call | solution.py:528

commit v5 on v4

--- a/solution.py
+++ b/solution.py
@@ -21,7 +21,7 @@
 VMEM_LIMIT = 67043328 - (1088 << 10)
 HALF = (BS, 2 * BS)
 REACH = (4, 3, 5, 2, 6, 1, 7)
-GROUPS = ((1, 7, 2, 6), (3, 5), (4,))
+GROUPS = ((2, 6, 1, 7), (3, 5), (4,))
 
 
 def dot(a, b):

time: 40.7 us -> 40.7 us (level)
  no operation moved by 1% of the time
where the time goes in v5:
time: 40.7 us; the launch traced here: 40.6 us
  Pallas kernels  38.6 us (95%)
  between operations  1.93 us (5%)
    pallas_call x1, Pallas kernels, per_device(): pl.pallas_call(kernel, name='galerkin', out_shape=(pltpu.VMEM((CB, 5, CB,...  37.5 us
    pallas_call x1, Pallas kernels, per_device(): pl.pallas_call(finish, name='finish', out_shape=(jax.ShapeDtypeStruct((CB...  1.13 us

profile of v5, /device:TPU:7, one launch (start us, length us, event | category | flops | bytes accessed | tf_op | source)
XLA Modules:
  0.0 40.6 jit_solution(16075963793027455116)
XLA Ops:
  1.9 37.5 %galerkin.1 = (bf16[2,5,2,128,128]{4,3,2,1,0:T(8,128)(2,1)S(1)}, bf16[2,8,16,256]{3,2,1,0:T(8,128)(2,1)S(1)}, bf16[2,8,32,256]{3,2,1,0:T(8,128)(2,1)S(1)}) custom-call(s32[1,1,64]{2,1,0:T(1,128)} %cols_hbm.1, s32[1,1,64]{2,1,0:T(1,128)} %rows_hbm.1, s32[1,1]{1,0:T(1,128)S(6)} %copy.11.fcount_s, s32[1,1,12]{2,1,0:T(1,128)} %codes_hbm.1, ...), custom_call_target="tpu_custom_call" | custom-call | tf_op jit(solution)/shard_map/galerkin/pallas_call | solution.py:463
  39.4 1.1 %finish.1 = (bf16[2,5,2,128,128]{4,3,2,1,0:T(8,128)(2,1)}, f32[2,3,2,128,128]{4,3,2,1,0:T(8,128)}) custom-call(bf16[2,5,2,128,128]{4,3,2,1,0:T(8,128)(2,1)S(1)} %get-tuple-element.7.one_v, bf16[2,8,16,256]{3,2,1,0:T(8,128)(2,1)S(1)} %get-tuple-element.8.early_v, bf16[2,8,32,256]{3,2,1,0:T(8,128)(2,1)S(1)} %get-tuple-element.9.late_v), custom_call_target="tpu_custom_call" | custom-call | tf_op jit(solution)/shard_map/finish/pallas_call | solution.py:528
